TPU v7x, 32 devices: a whole 2x2x4 slice. The times are simulated.
32 devices in a mesh: head: 2 (over y), ctx: 4 (over z), batch: 4 (over x, core).
Axes of the slice: x: 2, y: 2, z: 4, core: 2. Of those that a mesh axis runs over, the one named last changes fastest.
Arguments:
- tokens: bfloat16 [4, 1024, 1024], P('batch', ('ctx', 'head')), may hold values from -6 to 6
- cotangent: bfloat16 [4, 1024, 1024], P('batch', ('ctx', 'head')), may hold values from -6 to 6
- norm1_gain: bfloat16 [1024], P(('head', 'ctx', 'batch')), may hold values from 0.5 to 1.5
- w_query: bfloat16 [1024, 1024], P(('head', 'ctx', 'batch')), may hold values from -0.1875 to 0.1875
- w_key: bfloat16 [1024, 1024], P(('head', 'ctx', 'batch')), may hold values from -0.1875 to 0.1875
- w_value: bfloat16 [1024, 2048], P(('head', 'ctx', 'batch')), may hold values from -0.1875 to 0.1875
- w_gate: bfloat16 [1024, 2048], P(('head', 'ctx', 'batch')), may hold values from -0.1875 to 0.1875
- w_rates: bfloat16 [1024, 16], P(('head', 'ctx', 'batch')), may hold values from -0.1875 to 0.1875
- conv_query: bfloat16 [4, 1024], P(None, 'head'), may hold values from -3 to 3
- conv_key: bfloat16 [4, 1024], P(None, 'head'), may hold values from -3 to 3
- conv_value: bfloat16 [4, 2048], P(None, 'head'), may hold values from -3 to 3
- decay_log: float32 [8], P('head'), may hold values from -7 to 0.5
- decay_bias: float32 [8], P('head'), may hold values from -4 to 1
- out_gain: bfloat16 [2048], P('head'), may hold values from 0.5 to 1.5
- w_out: bfloat16 [1024, 2048], P(('head', 'ctx', 'batch')), may hold values from -0.125 to 0.125
- norm2_gain: bfloat16 [1024], P(('head', 'ctx', 'batch')), may hold values from 0.5 to 1.5
- w_ffgate: bfloat16 [1024, 2816], P(('head', 'ctx', 'batch')), may hold values from -0.1875 to 0.1875
- w_ffup: bfloat16 [1024, 2816], P(('head', 'ctx', 'batch')), may hold values from -0.1875 to 0.1875
- w_down: bfloat16 [1024, 2816], P(('head', 'ctx', 'batch')), may hold values from -0.109375 to 0.109375
Outputs:
- output: bfloat16 [4, 1024, 1024], P('batch', ('ctx', 'head'))
- input_grad: float32 [4, 1024, 1024], P('batch', ('ctx', 'head'))
- g_norm1: float32 [1024], P(('head', 'ctx', 'batch'))
- g_query: float32 [1024, 1024], P(('ctx', 'batch'), 'head')
- g_key: float32 [1024, 1024], P(('ctx', 'batch'), 'head')
- g_value: float32 [1024, 2048], P(('ctx', 'batch'), 'head')
- g_gate: float32 [1024, 2048], P(('ctx', 'batch'), 'head')
- g_rates: float32 [1024, 16], P(('ctx', 'batch'), 'head')
- g_conv_query: float32 [4, 1024], P(None, 'head')
- g_conv_key: float32 [4, 1024], P(None, 'head')
- g_conv_value: float32 [4, 2048], P(None, 'head')
- g_decay_log: float32 [8], P('head')
- g_decay_bias: float32 [8], P('head')
- g_out_gain: float32 [2048], P('head')
- g_out: float32 [1024, 2048], P(('ctx', 'batch'), 'head')
- g_norm2: float32 [1024], P(('head', 'ctx', 'batch'))
- g_ffgate: float32 [1024, 2816], P(('ctx', 'batch'), 'head')
- g_ffup: float32 [1024, 2816], P(('ctx', 'batch'), 'head')
- g_down: float32 [1024, 2816], P(('ctx', 'batch'), 'head')
All inputs are finite; a program needn't handle non-finite values.
Results may differ from a plain program's by a relative error of at most 0.02.
Values may be sent and summed in bfloat16 or wider, within the bound.
A program may use at most 256 MiB of HBM per device.

v0:
```python
import math

import jax
import jax.numpy as jnp
from jax import lax
from jax.sharding import PartitionSpec as P

DK = 128
DV = 256
KW = 4
SPAN = 64


epsilon = 1e-06
highest_precision = lax.Precision.HIGHEST


def passed_along(block, axis, distance):
    devices = range(lax.axis_size(axis))
    route = [(i - distance, i) for i in devices if i - distance in devices]
    return lax.ppermute(block, axis, route)


def mat_nt(first_mat, second_mat):
    return lax.dot_general(
        first_mat, second_mat, (((1,), (1,)), ((), ())), preferred_element_type=jnp.float32
    )


def mat_tn(first_mat, second_mat):
    return lax.dot_general(
        first_mat, second_mat, (((0,), (0,)), ((), ())), preferred_element_type=jnp.float32
    )


def rms_scale(hidden, gain_vec):
    return (
        hidden * lax.rsqrt(jnp.mean(hidden * hidden, axis=-1, keepdims=True) + epsilon) * gain_vec
    )


def swiglu(gate_part, up_part):
    return jax.nn.silu(gate_part) * up_part


def unit_rows(matrix):
    return matrix * lax.rsqrt(jnp.sum(matrix * matrix, axis=-1, keepdims=True) + epsilon)


def prepare(padded, conv_all, rates, decay_log, decay_bias):
    head_count = decay_log.shape[0]
    length = padded.shape[0] - (KW - 1)
    mixed_rows = padded[0:length] * conv_all[0]
    for tap_index in range(1, KW):
        mixed_rows = mixed_rows + padded[tap_index : tap_index + length] * conv_all[tap_index]
    active = jax.nn.silu(mixed_rows)
    split_one = head_count * DK
    queries = unit_rows(active[:, :split_one].reshape(length, head_count, DK)) / math.sqrt(DK)
    keys_vec = unit_rows(active[:, split_one : 2 * split_one].reshape(length, head_count, DK))
    values = active[:, 2 * split_one :].reshape(length, head_count, DV)
    rate_pairs = rates.reshape(length, head_count, 2)
    log_decay = -jnp.exp(decay_log) * jax.nn.softplus(rate_pairs[:, :, 0] + decay_bias)
    strength = jax.nn.sigmoid(rate_pairs[:, :, 1])
    return (queries, keys_vec, values, log_decay, strength)


def span_parts(keys_blk, values_blk, decay_blk, strength_blk):
    key_heads = jnp.transpose(keys_blk, (1, 0, 2))
    value_heads = jnp.transpose(values_blk, (1, 0, 2))
    cumulative = jnp.cumsum(jnp.transpose(decay_blk), axis=1)
    strength_heads = jnp.transpose(strength_blk)
    block_size = cumulative.shape[1]
    row_index = jnp.arange(block_size)[:, None]
    col_index = jnp.arange(block_size)[None, :]
    strict = row_index > col_index
    inclusive = row_index >= col_index
    gaps = cumulative[:, :, None] - cumulative[:, None, :]
    below_decay = jnp.where(strict, jnp.exp(jnp.where(strict, gaps, 0.0)), 0.0)
    key_gram = jnp.einsum("htd,hsd->hts", key_heads, key_heads, precision=highest_precision)
    system = (
        jnp.eye(block_size, dtype=jnp.float32) + strength_heads[:, :, None] * below_decay * key_gram
    )
    decay_factor = jnp.exp(cumulative)
    targets = jnp.concatenate(
        [
            strength_heads[:, :, None] * value_heads,
            (strength_heads * decay_factor)[:, :, None] * key_heads,
        ],
        axis=2,
    )
    solved = jax.scipy.linalg.solve_triangular(system, targets, lower=True, unit_diagonal=True)
    value_width = value_heads.shape[2]
    direct_term = solved[:, :, :value_width]
    across_devices_total = solved[:, :, value_width:]
    tail_decay = jnp.exp(cumulative[:, -1:] - cumulative)
    decayed_key_rows = tail_decay[:, :, None] * key_heads
    final_decay_factor = jnp.exp(cumulative[:, -1])
    within = jnp.where(inclusive, jnp.exp(jnp.where(inclusive, gaps, 0.0)), 0.0)
    return (
        key_heads,
        decay_factor,
        within,
        direct_term,
        across_devices_total,
        decayed_key_rows,
        final_decay_factor,
    )


def delta_block(incoming_state, block_in):
    query_blk, keys_blk, values_blk, decay_blk, strength_blk = block_in
    (
        key_heads,
        decay_factor,
        within,
        direct_term,
        across_devices_total,
        decayed_key_rows,
        final_decay_factor,
    ) = span_parts(keys_blk, values_blk, decay_blk, strength_blk)
    query_head_rows = jnp.transpose(query_blk, (1, 0, 2))
    state_update = direct_term - jnp.einsum(
        "nal,nlr->nar", across_devices_total, incoming_state, precision=highest_precision
    )
    scores = (
        jnp.einsum("htd,hsd->hts", query_head_rows, key_heads, precision=highest_precision) * within
    )
    layer_result = decay_factor[:, :, None] * jnp.einsum(
        "nal,nlr->nar", query_head_rows, incoming_state, precision=highest_precision
    )
    layer_result = layer_result + jnp.einsum(
        "hts,hsv->htv", scores, state_update, precision=highest_precision
    )
    updated_state = final_decay_factor[:, None, None] * incoming_state + jnp.einsum(
        "pex,ped->pxd", decayed_key_rows, state_update, precision=highest_precision
    )
    return (updated_state, jnp.transpose(layer_result, (1, 0, 2)))


def into_blocks(tensor):
    return tensor.reshape((tensor.shape[0] // SPAN, SPAN) + tensor.shape[1:])


def mixer_out(queries, keys_vec, values, log_decay, strength, initial_state):
    final_state, outputs = lax.scan(
        delta_block,
        initial_state,
        (
            into_blocks(queries),
            into_blocks(keys_vec),
            into_blocks(values),
            into_blocks(log_decay),
            into_blocks(strength),
        ),
    )
    return outputs.reshape((queries.shape[0],) + outputs.shape[2:])


def transition_block(carry_in, block_in):
    state_map, state_offset = carry_in
    keys_blk, values_blk, decay_blk, strength_blk = block_in
    (
        key_heads,
        decay_factor,
        within,
        direct_term,
        across_devices_total,
        decayed_key_rows,
        final_decay_factor,
    ) = span_parts(keys_blk, values_blk, decay_blk, strength_blk)
    identity_stack = jnp.eye(key_heads.shape[2], dtype=jnp.float32)[None]
    local_map = final_decay_factor[:, None, None] * identity_stack - jnp.einsum(
        "hsk,hsj->hkj", decayed_key_rows, across_devices_total, precision=highest_precision
    )
    local_state_shift = jnp.einsum(
        "pex,ped->pxd", decayed_key_rows, direct_term, precision=highest_precision
    )
    new_map = jnp.einsum("hij,hjk->hik", local_map, state_map, precision=highest_precision)
    new_offset = (
        jnp.einsum("hij,hjv->hiv", local_map, state_offset, precision=highest_precision)
        + local_state_shift
    )
    return ((new_map, new_offset), None)


def transition(keys_vec, values, log_decay, strength):
    head_count = keys_vec.shape[1]
    key_width = keys_vec.shape[2]
    start_map = jnp.broadcast_to(
        jnp.eye(key_width, dtype=jnp.float32), (head_count, key_width, key_width)
    )
    start_offset = jnp.zeros((head_count, key_width, values.shape[2]), jnp.float32)
    final_carry, unused_rows = lax.scan(
        transition_block,
        (start_map, start_offset),
        (into_blocks(keys_vec), into_blocks(values), into_blocks(log_decay), into_blocks(strength)),
    )
    return final_carry


def apply_map(state_map, state_offset, incoming_state):
    return (
        jnp.einsum("hij,hjv->hiv", state_map, incoming_state, precision=highest_precision)
        + state_offset
    )


def out_gate(mixer_rows, gate_rows, gain_vec):
    normed = mixer_rows * lax.rsqrt(
        jnp.mean(mixer_rows * mixer_rows, axis=-1, keepdims=True) + epsilon
    )
    flat = normed.reshape(mixer_rows.shape[0], mixer_rows.shape[1] * mixer_rows.shape[2])
    return flat * gain_vec * jax.nn.silu(gate_rows)


def split_columns(matrix, widths):
    pieces = []
    offset_col = 0
    for width_one in widths:
        pieces.append(matrix[:, offset_col : offset_col + width_one])
        offset_col = offset_col + width_one
    return pieces


def body(
    tokens,
    cotangent,
    norm1_gain,
    w_query,
    w_key,
    w_value,
    w_gate,
    w_rates,
    conv_query,
    conv_key,
    conv_value,
    decay_log,
    decay_bias,
    out_gain,
    w_out,
    norm2_gain,
    w_ffgate,
    w_ffup,
    w_down,
):
    (
        gain_one,
        query_weight,
        key_weight,
        value_weight,
        gate_weight,
        rates_weight,
        out_weight,
        gain_two,
        ffgate_weight,
        ffup_weight,
        down_weight,
    ) = (
        lax.all_gather(norm1_gain, ("head", "ctx", "batch"), axis=0, tiled=True),
        lax.all_gather(w_query, ("head", "ctx", "batch"), axis=0, tiled=True),
        lax.all_gather(w_key, ("head", "ctx", "batch"), axis=0, tiled=True),
        lax.all_gather(w_value, ("head", "ctx", "batch"), axis=0, tiled=True),
        lax.all_gather(w_gate, ("head", "ctx", "batch"), axis=0, tiled=True),
        lax.all_gather(w_rates, ("head", "ctx", "batch"), axis=0, tiled=True),
        lax.all_gather(w_out, ("head", "ctx", "batch"), axis=0, tiled=True),
        lax.all_gather(norm2_gain, ("head", "ctx", "batch"), axis=0, tiled=True),
        lax.all_gather(w_ffgate, ("head", "ctx", "batch"), axis=0, tiled=True),
        lax.all_gather(w_ffup, ("head", "ctx", "batch"), axis=0, tiled=True),
        lax.all_gather(w_down, ("head", "ctx", "batch"), axis=0, tiled=True),
    )
    inputs_tok = tokens[0]
    cot_tok = cotangent[0]
    residual = inputs_tok.astype(jnp.float32)
    normed_f, norm_one_vjp = jax.vjp(rms_scale, residual, gain_one.astype(jnp.float32))
    normed_one = normed_f.astype(jnp.bfloat16)
    query_raw = jnp.dot(normed_one, query_weight, preferred_element_type=jnp.float32).astype(
        jnp.bfloat16
    )
    key_raw = jnp.dot(normed_one, key_weight, preferred_element_type=jnp.float32).astype(
        jnp.bfloat16
    )
    value_raw = jnp.dot(normed_one, value_weight, preferred_element_type=jnp.float32).astype(
        jnp.bfloat16
    )
    gate_raw = jnp.dot(normed_one, gate_weight, preferred_element_type=jnp.float32).astype(
        jnp.bfloat16
    )
    rates_raw = jnp.dot(normed_one, rates_weight, preferred_element_type=jnp.float32).astype(
        jnp.bfloat16
    )
    query_here, key_here, value_here, gate_here, rates_here = (
        lax.all_to_all(query_raw, "head", split_axis=1, concat_axis=0, tiled=True),
        lax.all_to_all(key_raw, "head", split_axis=1, concat_axis=0, tiled=True),
        lax.all_to_all(value_raw, "head", split_axis=1, concat_axis=0, tiled=True),
        lax.all_to_all(gate_raw, "head", split_axis=1, concat_axis=0, tiled=True),
        lax.all_to_all(rates_raw, "head", split_axis=1, concat_axis=0, tiled=True),
    )
    joined = jnp.concatenate([query_here, key_here, value_here], axis=1)
    margin = KW - 1
    piece_rows = joined.shape[0]
    rim_rows = passed_along(joined[piece_rows - margin :], "ctx", 1)
    padded = jnp.concatenate([rim_rows, joined], axis=0).astype(jnp.float32)
    conv_all = jnp.concatenate([conv_query, conv_key, conv_value], axis=1).astype(jnp.float32)
    prepared, prepare_vjp = jax.vjp(
        prepare, padded, conv_all, rates_here.astype(jnp.float32), decay_log, decay_bias
    )
    queries, keys_vec, values, log_decay, strength = prepared
    chain_maps, transition_vjp = jax.vjp(transition, keys_vec, values, log_decay, strength)
    state_map, state_offset = chain_maps
    zero_state = jnp.zeros_like(state_offset)

    def relay_step(step_index, incoming_state):
        return passed_along(
            apply_map(state_map, state_offset, incoming_state).astype(jnp.bfloat16), "ctx", 1
        ).astype(jnp.float32)

    initial_state = lax.fori_loop(0, lax.axis_size("ctx") - 1, relay_step, zero_state)
    mixer_rows, mixer_vjp = jax.vjp(
        mixer_out, queries, keys_vec, values, log_decay, strength, initial_state
    )
    gated_f, gate_vjp = jax.vjp(
        out_gate, mixer_rows, gate_here.astype(jnp.float32), out_gain.astype(jnp.float32)
    )
    gated_here = gated_f.astype(jnp.bfloat16)
    gated_tok = lax.all_to_all(gated_here, "head", split_axis=0, concat_axis=1, tiled=True)
    middle = residual + mat_nt(gated_tok, out_weight)
    normed_two_f, norm_two_vjp = jax.vjp(rms_scale, middle, gain_two.astype(jnp.float32))
    normed_two = normed_two_f.astype(jnp.bfloat16)
    ff_gate = jnp.dot(normed_two, ffgate_weight, preferred_element_type=jnp.float32)
    ff_up = jnp.dot(normed_two, ffup_weight, preferred_element_type=jnp.float32)
    hidden_f, swiglu_vjp = jax.vjp(swiglu, ff_gate, ff_up)
    hidden = hidden_f.astype(jnp.bfloat16)
    output_tok = (middle + mat_nt(hidden, down_weight)).astype(jnp.bfloat16)
    hidden_grad = jnp.dot(cot_tok, down_weight, preferred_element_type=jnp.float32)
    gate_grad_f, up_grad_f = swiglu_vjp(hidden_grad)
    ffgate_grad = gate_grad_f.astype(jnp.bfloat16)
    ffup_grad = up_grad_f.astype(jnp.bfloat16)
    normed_two_grad = mat_nt(ffgate_grad, ffgate_weight) + mat_nt(ffup_grad, ffup_weight)
    middle_part, gain_two_grad = norm_two_vjp(normed_two_grad)
    middle_grad = cot_tok.astype(jnp.float32) + middle_part
    middle_grad_b = middle_grad.astype(jnp.bfloat16)
    gated_grad_tok = jnp.dot(middle_grad_b, out_weight, preferred_element_type=jnp.float32).astype(
        jnp.bfloat16
    )
    piece_normed_one, piece_midgrad, piece_normed_two, piece_cot = (
        lax.all_gather(normed_one, "head", axis=0, tiled=True),
        lax.all_gather(middle_grad_b, "head", axis=0, tiled=True),
        lax.all_gather(normed_two, "head", axis=0, tiled=True),
        lax.all_gather(cot_tok, "head", axis=0, tiled=True),
    )
    ffgate_cols, ffup_cols, hidden_cols = (
        lax.all_to_all(ffgate_grad, "head", split_axis=1, concat_axis=0, tiled=True),
        lax.all_to_all(ffup_grad, "head", split_axis=1, concat_axis=0, tiled=True),
        lax.all_to_all(hidden, "head", split_axis=1, concat_axis=0, tiled=True),
    )
    ff_local = ffgate_cols.shape[1]
    gated_grad = lax.all_to_all(gated_grad_tok, "head", split_axis=1, concat_axis=0, tiled=True)
    mixer_grad, gate_grad_here, out_gain_grad = gate_vjp(gated_grad.astype(jnp.float32))
    query_g, key_g_one, value_g_one, decay_g_one, strength_g_one, reach = mixer_vjp(mixer_grad)

    def relay_back(step_index, grad_in):
        return passed_along(
            (
                jnp.einsum("hji,hjv->hiv", state_map, grad_in, precision=highest_precision) + reach
            ).astype(jnp.bfloat16),
            "ctx",
            -1,
        ).astype(jnp.float32)

    final_state_gradient = lax.fori_loop(
        0, lax.axis_size("ctx") - 1, relay_back, jnp.zeros_like(reach)
    )
    map_gradient = jnp.einsum(
        "zwx,zfx->zwf", final_state_gradient, initial_state, precision=highest_precision
    )
    key_g_two, value_g_two, decay_g_two, strength_g_two = transition_vjp(
        (map_gradient, final_state_gradient)
    )
    padded_grad, conv_grad, rates_grad_f, decay_log_grad, decay_bias_grad = prepare_vjp(
        (
            query_g,
            key_g_one + key_g_two,
            value_g_one + value_g_two,
            decay_g_one + decay_g_two,
            strength_g_one + strength_g_two,
        )
    )
    back_rim = passed_along(padded_grad[:margin], "ctx", -1)
    own_rows = padded_grad[margin:]
    own_rows = jnp.concatenate(
        [own_rows[: piece_rows - margin], own_rows[piece_rows - margin :] + back_rim], axis=0
    ).astype(jnp.bfloat16)
    query_width = query_here.shape[1]
    gate_bf = gate_grad_here.astype(jnp.bfloat16)
    rates_bf = rates_grad_f.astype(jnp.bfloat16)
    query_field = own_rows[:, :query_width]
    key_field = own_rows[:, query_width : 2 * query_width]
    value_field = own_rows[:, 2 * query_width :]
    query_back, key_back, value_back, gate_back, rates_back = (
        lax.all_to_all(query_field, "head", split_axis=0, concat_axis=1, tiled=True),
        lax.all_to_all(key_field, "head", split_axis=0, concat_axis=1, tiled=True),
        lax.all_to_all(value_field, "head", split_axis=0, concat_axis=1, tiled=True),
        lax.all_to_all(gate_bf, "head", split_axis=0, concat_axis=1, tiled=True),
        lax.all_to_all(rates_bf, "head", split_axis=0, concat_axis=1, tiled=True),
    )
    summed = lax.psum(
        (
            conv_grad[:, :query_width],
            conv_grad[:, query_width : 2 * query_width],
            conv_grad[:, 2 * query_width :],
            decay_log_grad,
            decay_bias_grad,
            out_gain_grad,
        ),
        ("ctx", "batch"),
    )
    mixer_widths = (
        query_width,
        query_width,
        value_field.shape[1],
        gate_bf.shape[1],
        rates_bf.shape[1],
        gated_here.shape[1],
    )
    mixer_total = sum(mixer_widths)
    joined_sums = lax.psum_scatter(
        jnp.concatenate(
            [
                jnp.concatenate(
                    [
                        mat_tn(piece_normed_one, query_field),
                        mat_tn(piece_normed_one, key_field),
                        mat_tn(piece_normed_one, value_field),
                        mat_tn(piece_normed_one, gate_bf),
                        mat_tn(piece_normed_one, rates_bf),
                        mat_tn(piece_midgrad, gated_here),
                    ],
                    axis=1,
                ),
                jnp.concatenate(
                    [
                        mat_tn(piece_normed_two, ffgate_cols),
                        mat_tn(piece_normed_two, ffup_cols),
                        mat_tn(piece_cot, hidden_cols),
                    ],
                    axis=1,
                ),
            ],
            axis=1,
        ).astype(jnp.bfloat16),
        ("ctx", "batch"),
        scatter_dimension=0,
        tiled=True,
    ).astype(jnp.float32)
    mixer_sums = joined_sums[:, :mixer_total]
    ff_rows = joined_sums[:, mixer_total:]
    mixer_parts = split_columns(mixer_sums, mixer_widths)
    ff_parts = split_columns(ff_rows, (ff_local, ff_local, ff_local))
    normed_one_grad = (
        mat_nt(query_back, query_weight)
        + mat_nt(key_back, key_weight)
        + mat_nt(value_back, value_weight)
        + mat_nt(gate_back, gate_weight)
        + mat_nt(rates_back, rates_weight)
    )
    input_part, gain_one_grad = norm_one_vjp(normed_one_grad)
    input_grad = middle_grad + input_part
    gain_sums = (
        lax.psum_scatter(gain_one_grad, ("head", "ctx", "batch"), scatter_dimension=0, tiled=True),
        lax.psum_scatter(gain_two_grad, ("head", "ctx", "batch"), scatter_dimension=0, tiled=True),
    )
    return (
        output_tok[None],
        input_grad[None],
        gain_sums[0],
        mixer_parts[0],
        mixer_parts[1],
        mixer_parts[2],
        mixer_parts[3],
        mixer_parts[4],
        summed[0],
        summed[1],
        summed[2],
        summed[3],
        summed[4],
        summed[5],
        mixer_parts[5],
        gain_sums[1],
        ff_parts[0],
        ff_parts[1],
        ff_parts[2],
    )


def solution(mesh):
    placed = (
        P("batch", ("ctx", "head"), None),
        P("batch", ("ctx", "head"), None),
        P(("head", "ctx", "batch")),
        P(("head", "ctx", "batch"), None),
        P(("head", "ctx", "batch"), None),
        P(("head", "ctx", "batch"), None),
        P(("head", "ctx", "batch"), None),
        P(("head", "ctx", "batch"), None),
        P(None, "head"),
        P(None, "head"),
        P(None, "head"),
        P("head"),
        P("head"),
        P("head"),
        P(("head", "ctx", "batch"), None),
        P(("head", "ctx", "batch")),
        P(("head", "ctx", "batch"), None),
        P(("head", "ctx", "batch"), None),
        P(("head", "ctx", "batch"), None),
    )
    return jax.shard_map(
        body,
        mesh=mesh,
        in_specs=placed,
        out_specs=(
            P("batch", ("ctx", "head"), None),
            P("batch", ("ctx", "head"), None),
            P(("head", "ctx", "batch")),
            P(("ctx", "batch"), "head"),
            P(("ctx", "batch"), "head"),
            P(("ctx", "batch"), "head"),
            P(("ctx", "batch"), "head"),
            P(("ctx", "batch"), "head"),
            P(None, "head"),
            P(None, "head"),
            P(None, "head"),
            P("head"),
            P("head"),
            P("head"),
            P(("ctx", "batch"), "head"),
            P(("head", "ctx", "batch")),
            P(("ctx", "batch"), "head"),
            P(("ctx", "batch"), "head"),
            P(("ctx", "batch"), "head"),
        ),
        check_vma=False,
    )
```

profile of v0, /device:TPU:0, one launch (start us, length us, event | category | flops | bytes accessed | tf_op | source)
XLA Modules:
  0.0 1612.0 jit_solution(101802768778225533)
XLA Ops:
  13.7 42.0 %all-reduce.27 = (bf16[1024]{0:T(1024)(128)(2,1)S(1)}, bf16[1024]{0:T(1024)(128)(2,1)S(1)}) all-reduce(bf16[1024]{0:T(1024)(128)(2,1)S(1)} %dynamic-update-slice, bf16[1024]{0:T(1024)(128)(2,1)S(1)} %dynamic-update-slice.1), channel_id=1, replica_groups=mesh['head'=2,'ctx'=4,'batch'=4] {'head','ctx','batch'}, use_global_device_ids=true, to_apply=%add.21 | all-reduce | flops 2048 | bytes 8192
  55.7 40.9 %all-gather.1 = bf16[32,32,16]{1,2,0:T(8,128)(2,1)S(1)} all-gather(bf16[1,32,16]{1,2,0:T(8,128)(2,1)} %bitcast.1194), channel_id=1, replica_groups=mesh['head'=2,'ctx'=4,'batch'=4] {'head','ctx','batch'}, dimensions={0}, use_global_device_ids=true | all-gather | bytes 33792 | tf_op jit(solution)/shard_map/all_gather | solution.py:264
  140.5 52.8 %all-gather.15.cloned.1.call-done = bf16[1024,2048]{1,0:T(8,128)(2,1)} async-done(((bf16[32,2048]{1,0:T(8,128)(2,1)}), bf16[1024,2048]{1,0:T(8,128)(2,1)}) %all-gather.15.cloned.1.call-update) | async-done | bytes 4194320 | tf_op jit(solution)/shard_map/all_gather | solution.py:262
  214.1 42.9 %all-gather.17.cloned.1.call-done = bf16[1024,2048]{1,0:T(8,128)(2,1)} async-done(((bf16[32,2048]{1,0:T(8,128)(2,1)}), bf16[1024,2048]{1,0:T(8,128)(2,1)}) %all-gather.17.cloned.1.call-update) | async-done | bytes 4194320 | tf_op jit(solution)/shard_map/all_gather | solution.py:263
  307.2 159.6 %while.214 = (s32[]{:T(128)}, f32[4,128,128]{2,1,0:T(8,128)}, f32[4,128,256]{2,1,0:T(8,128)S(1)}, f32[4,4,64,64]{3,2,1,0:T(8,128)}, f32[4,4,64,128]{3,2,1,0:T(8,...) while((s32[]{:T(128)}, f32[4,128,128]{2,1,0:T(8,128)}, ...), condition=%wide.region_4.6_spmd.clone.clone, body=%wide.region_2.5_spmd.clone.clone.sunk | while | flops 554832704 | bytes 17746580 | solution.py:193
  312.0 20.4 %custom-call.27 = f32[4,1,64,64]{2,3,1,0:T(8,128)S(1)} custom-call(f32[4,1,64,64]{3,2,1,0:T(8,128)} %add_bitcast_fusion.5), custom_call_target="InvertDiagBlocksLowerTriangular" | custom-call | tf_op jit(solution)/shard_map/jvp()/while/body/eval_jaxpr/jit(_solve_triangular)/vmap()/triangular_solve | solution.py:91
  351.9 20.4 %custom-call.27 = f32[4,1,64,64]{2,3,1,0:T(8,128)S(1)} custom-call(f32[4,1,64,64]{3,2,1,0:T(8,128)} %add_bitcast_fusion.5), custom_call_target="InvertDiagBlocksLowerTriangular" | custom-call | tf_op jit(solution)/shard_map/jvp()/while/body/eval_jaxpr/jit(_solve_triangular)/vmap()/triangular_solve | solution.py:91
  467.4 52.6 %while.212 = (s32[]{:T(128)}, f32[4,128,256]{2,1,0:T(8,128)}, f32[4,128,128]{2,1,0:T(8,128)}, f32[4,128,256]{2,1,0:T(8,128)S(1)}, s32[]{:T(128)}, /*index=5*/s32[]{:T(128)}) while((s32[]{:T(128)}, f32[4,128,256]{2,1,0:T(8,128)}, f32[4,128,128]{2,1,0:T(8,128)}, f32[4,128,256]{2,1,0:T(8,128)S(1)}, s32[]{:T(128)}, ...), condition=%wide.region_6.8_spmd.clone, body=%wide.region_5.7_spmd.clone.sunk | while | flops 201850880 | bytes 3407991 | solution.py:317
  544.4 167.0 %while.210 = (s32[]{:T(128)}, f32[4,128,256]{2,1,0:T(8,128)S(1)}, f32[4,64,4,256]{3,1,2,0:T(8,128)}, f32[4,4,64,64]{3,2,1,0:T(8,128)}, f32[4,4,64,128]{3,2,1,0:T...) while((s32[]{:T(128)}, f32[4,128,256]{2,1,0:T(8,128)S(1)}, ...), condition=%wide.region_10.12_spmd.clone.clone, body=%wide.region_8.11_spmd.clone.clone.sunk | while | flops 479351616 | bytes 16081781 | solution.py:145
  550.0 21.0 %custom-call.25 = f32[4,1,64,64]{2,3,1,0:T(8,128)} custom-call(f32[4,1,64,64]{3,2,1,0:T(8,128)} %add_bitcast_fusion.4), custom_call_target="InvertDiagBlocksLowerTriangular" | custom-call | tf_op jit(solution)/shard_map/jvp()/while/body/eval_jaxpr/jit(_solve_triangular)/vmap()/triangular_solve | solution.py:91
  591.8 21.0 %custom-call.25 = f32[4,1,64,64]{2,3,1,0:T(8,128)} custom-call(f32[4,1,64,64]{3,2,1,0:T(8,128)} %add_bitcast_fusion.4), custom_call_target="InvertDiagBlocksLowerTriangular" | custom-call | tf_op jit(solution)/shard_map/jvp()/while/body/eval_jaxpr/jit(_solve_triangular)/vmap()/triangular_solve | solution.py:91
  633.5 21.0 %custom-call.25 = f32[4,1,64,64]{2,3,1,0:T(8,128)} custom-call(f32[4,1,64,64]{3,2,1,0:T(8,128)} %add_bitcast_fusion.4), custom_call_target="InvertDiagBlocksLowerTriangular" | custom-call | tf_op jit(solution)/shard_map/jvp()/while/body/eval_jaxpr/jit(_solve_triangular)/vmap()/triangular_solve | solution.py:91
  675.3 21.0 %custom-call.25 = f32[4,1,64,64]{2,3,1,0:T(8,128)} custom-call(f32[4,1,64,64]{3,2,1,0:T(8,128)} %add_bitcast_fusion.4), custom_call_target="InvertDiagBlocksLowerTriangular" | custom-call | tf_op jit(solution)/shard_map/jvp()/while/body/eval_jaxpr/jit(_solve_triangular)/vmap()/triangular_solve | solution.py:91
  816.1 241.1 %while.215 = (s32[]{:T(128)}, f32[4,128,256]{2,1,0:T(8,128)S(1)}, f32[4,64,4,128]{3,1,2,0:T(8,128)}, f32[4,64,4,128]{3,1,0,2:T(8,128)}, f32[4,64,4,256]{3,1,2,0:...) while((s32[]{:T(128)}, f32[4,128,256]{2,1,0:T(8,128)S(1)}, ...), condition=%wide.region_26.29_spmd.clone.clone, body=%wide.region_15.28_spmd.clone.clone.sunk | while | flops 971667520 | bytes 20097464 | solution.py:145
  827.5 21.0 %custom-call.28 = f32[4,1,64,64]{2,3,1,0:T(8,128)} custom-call(f32[4,1,64,64]{3,2,1,0:T(8,128)} %fusion.627), custom_call_target="InvertDiagBlocksLowerTriangular" | custom-call | tf_op jit(solution)/shard_map/transpose(jvp())/while/body/eval_jaxpr/jit(_solve_triangular)/vmap()/triangular_solve | solution.py:91
  887.7 21.0 %custom-call.28 = f32[4,1,64,64]{2,3,1,0:T(8,128)} custom-call(f32[4,1,64,64]{3,2,1,0:T(8,128)} %fusion.627), custom_call_target="InvertDiagBlocksLowerTriangular" | custom-call | tf_op jit(solution)/shard_map/transpose(jvp())/while/body/eval_jaxpr/jit(_solve_triangular)/vmap()/triangular_solve | solution.py:91
  948.1 21.0 %custom-call.28 = f32[4,1,64,64]{2,3,1,0:T(8,128)} custom-call(f32[4,1,64,64]{3,2,1,0:T(8,128)} %fusion.627), custom_call_target="InvertDiagBlocksLowerTriangular" | custom-call | tf_op jit(solution)/shard_map/transpose(jvp())/while/body/eval_jaxpr/jit(_solve_triangular)/vmap()/triangular_solve | solution.py:91
  1008.3 21.0 %custom-call.28 = f32[4,1,64,64]{2,3,1,0:T(8,128)} custom-call(f32[4,1,64,64]{3,2,1,0:T(8,128)} %fusion.627), custom_call_target="InvertDiagBlocksLowerTriangular" | custom-call | tf_op jit(solution)/shard_map/transpose(jvp())/while/body/eval_jaxpr/jit(_solve_triangular)/vmap()/triangular_solve | solution.py:91
  1061.4 45.1 %while.213 = (s32[]{:T(128)}, f32[4,128,256]{2,1,0:T(8,128)S(1)}, f32[4,128,128]{1,2,0:T(8,128)S(1)}, f32[4,128,256]{2,1,0:T(8,128)S(1)}, s32[]{:T(128)}, /*index=5*/s32[]{:T(128)}) while((s32[]{:T(128)}, f32[4,128,256]{2,1,0:T(8,128)S(1)}, f32[4,128,128]{1,2,0:T(8,128)S(1)}, f32[4,128,256]{2,1,0:T(8,128)S(1)}, s32[]{:T(128)}, ...), condition=%wide.region_28.31_spmd.clone, body=%wide.region_27.30_spmd.clone.sunk | while | flops 201850880 | bytes 3407991 | solution.py:370
  1111.5 201.1 %while.211 = (s32[]{:T(128)}, f32[4,128,128]{2,1,0:T(8,128)}, f32[4,128,256]{2,1,0:T(8,128)S(1)}, f32[4,64,4,128]{3,1,0,2:T(8,128)}, f32[4,64,4,256]{3,1,2,0:T(8...) while((s32[]{:T(128)}, f32[4,128,128]{2,1,0:T(8,128)}, ...), condition=%wide.region_39.42_spmd.clone.clone, body=%wide.region_29.41_spmd.clone.clone.sunk | while | flops 1121236992 | bytes 23946008 | solution.py:193
  1382.0 32.2 %concatenate.35 = bf16[1024,8328]{1,0:T(8,128)(2,1)} concatenate(bf16[1024,512]{1,0:T(8,128)(2,1)} %copy.503, bf16[1024,512]{1,0:T(8,128)(2,1)} %copy.504, bf16[1024,1024]{1,0:T(8,128)(2,1)} %copy.505, bf16[1024,1024]{1,0:T(8,128)(2,1)} %copy.506, bf16[1024,8]{1,0:T(8,128)(2,1)} %copy.507, bf16[1024,1024]{1,0:T(8,128)(2,1)S(1)} %copy-done.32, ...), dimensions={1} | concatenate | bytes 34111488 | tf_op jit(solution)/shard_map/concatenate | solution.py:427
  1439.1 62.4 %all-reduce.26 = (f32[4,512]{1,0:T(4,128)}, f32[4,512]{1,0:T(4,128)}, f32[4,1024]{1,0:T(4,128)}, f32[4]{0:T(128)}, f32[4]{0:T(128)}, /*index=5*/f32[1024]{0:T(1024)}) all-reduce(f32[4,512]{1,0:T(4,128)S(1)} %get-tuple-element.4782, ...), channel_id=1, replica_groups=mesh['head'=2,'ctx'=4,'batch'=4] {'ctx','batch'}, use_global_device_ids=true, to_apply=%region_50.53 | all-reduce | flops 9224 | bytes 73792 | tf_op jit(solution)/shard_map/psum | solution.py:406
  1532.1 38.0 %all-reduce.25 = (f32[1024]{0:T(1024)S(1)}, f32[1024]{0:T(1024)S(1)}) all-reduce(f32[1024]{0:T(1024)S(1)} %get-tuple-element.4373, f32[1024]{0:T(1024)S(1)} %copy-done.124), channel_id=3, replica_groups=mesh['head'=2,'ctx'=4,'batch'=4] {'head','ctx','batch'}, use_global_device_ids=true, to_apply=%region_44.47.clone | all-reduce | flops 2048 | bytes 16384
  1572.4 27.2 %reduce-scatter.2.cloned.1.call-done = bf16[64,8328]{1,0:T(8,128)(2,1)} async-done(((bf16[1024,8328]{1,0:T(8,128)(2,1)}), bf16[64,8328]{1,0:T(8,128)(2,1)}) %reduce-scatter.2.cloned.1.call-update) | async-done | bytes 1066000 | tf_op jit(solution)/shard_map/reduce_scatter | solution.py:426
  (1296 shorter events, 1045.7 us)
Async XLA Ops:
  7.2 118.2 %all-gather.11.cloned.1.call-start = ((), (), s32[]{:S(2)}) async-start(), calls=%async_computation.16 | async-start | bytes 2162688 | tf_op jit(solution)/shard_map/all_gather | solution.py:260
  8.0 123.7 %all-gather.13.cloned.1.call-start = ((), (), s32[]{:S(2)}) async-start(), calls=%async_computation.17 | async-start | bytes 2162688 | tf_op jit(solution)/shard_map/all_gather | solution.py:261
  8.7 184.6 %all-gather.15.cloned.1.call-start = ((), (), s32[]{:S(2)}) async-start(), calls=%async_computation.18 | async-start | bytes 4325376 | tf_op jit(solution)/shard_map/all_gather | solution.py:262
  9.5 247.6 %all-gather.17.cloned.1.call-start = ((), (), s32[]{:S(2)}) async-start(), calls=%async_computation.19 | async-start | bytes 4325376 | tf_op jit(solution)/shard_map/all_gather | solution.py:263
  10.0 731.4 %all-gather.19.cloned.1.call-start = ((), (), s32[]{:S(2)}) async-start(), calls=%async_computation.20 | async-start | bytes 4325376 | tf_op jit(solution)/shard_map/all_gather | solution.py:265
  10.6 735.0 %all-gather.21.cloned.1.call-start = ((), (), s32[]{:S(2)}) async-start(), calls=%async_computation.21 | async-start | bytes 5947392 | tf_op jit(solution)/shard_map/all_gather | solution.py:267
  11.2 739.1 %all-gather.23.cloned.1.call-start = ((), (), s32[]{:S(2)}) async-start(), calls=%async_computation.22 | async-start | bytes 5947392 | tf_op jit(solution)/shard_map/all_gather | solution.py:268
  99.8 25.4 %all-to-all-start = ((bf16[128,2,8]{0,2,1:T(8,128)(2,1)}), bf16[128,2,8]{0,2,1:T(8,128)(2,1)S(1)}, u32[]{:S(2)}, u32[]{:S(2)}) async-start(bf16[128,2,8]{0,2,1:T(8,128)(2,1)} %fusion.304), calls=%async_computation | async-start | bytes 8192 | tf_op jit(solution)/shard_map/all_to_all | solution.py:296
  103.1 652.0 %all-gather.25.cloned.1.call-start = ((), (), s32[]{:S(2)}) async-start(), calls=%async_computation.23 | async-start | bytes 5947392 | tf_op jit(solution)/shard_map/all_gather | solution.py:269
  137.0 60.1 %all-to-all-start.2 = ((bf16[128,2,512]{2,0,1:T(8,128)(2,1)}), bf16[128,2,512]{2,0,1:T(8,128)(2,1)S(1)}, u32[]{:S(2)}, u32[]{:S(2)}) async-start(bf16[128,2,512]{2,0,1:T(8,128)(2,1)} %bitcast.829), calls=%async_computation.2 | async-start | bytes 524288 | tf_op jit(solution)/shard_map/all_to_all | solution.py:293
  197.1 13.1 all-to-all-start.3
  210.2 54.9 %collective-permute-start.2 = (bf16[3,2048]{1,0:T(4,128)(2,1)S(1)}, bf16[3,2048]{1,0:T(4,128)(2,1)}, u32[]{:S(2)}, u32[]{:S(2)}) collective-permute-start(bf16[3,2048]{1,0:T(4,128)(2,1)S(1)} %pad_maximum_fusion.3), channel_id=1, source_target_pairs={{0,4},{4,8},{8,12},{1,5},{5,9},{9,13},{2,6},{6,10},{10,14},{3,7},{... | collective-permute-start | bytes 36872 | tf_op jit(solution)/shard_map/ppermute | solution.py:21
  260.8 462.1 %all-to-all-start.4 = ((bf16[128,2,1024]{2,0,1:T(8,128)(2,1)}), bf16[128,2,1024]{2,0,1:T(8,128)(2,1)}, u32[]{:S(2)}, u32[]{:S(2)}) async-start(bf16[128,2,1024]{2,0,1:T(8,128)(2,1)} %bitcast.827), calls=%async_computation.4 | async-start | bytes 1048576 | tf_op jit(solution)/shard_map/all_to_all | solution.py:295
  469.6 12.2 collective-permute-start
  485.1 15.6 collective-permute-start
  504.0 15.1 collective-permute-start
  725.8 13.7 all-to-all-start.5
  770.5 25.8 %all-to-all-start.6 = ((bf16[128,2,1024]{2,0,1:T(8,128)(2,1)}), bf16[128,2,1024]{2,0,1:T(8,128)(2,1)S(1)}, u32[]{:S(2)}, u32[]{:S(2)}) async-start(bf16[128,2,1024]{2,0,1:T(8,128)(2,1)} %bitcast.1159), calls=%async_computation.6 | async-start | bytes 1048576 | tf_op jit(solution)/shard_map/all_to_all | solution.py:357
  796.3 556.3 %all-to-all-start.13 = ((bf16[128,2,1408]{2,0,1:T(8,128)(2,1)}), bf16[128,2,1408]{2,0,1:T(8,128)(2,1)}, u32[]{:S(2)}, u32[]{:S(2)}) async-start(bf16[128,2,1408]{2,0,1:T(8,128)(2,1)} %bitcast.1140), calls=%async_computation.13 | async-start | bytes 1441792 | tf_op jit(solution)/shard_map/all_to_all | solution.py:353
  1062.7 19.3 %collective-permute-start.1 = (bf16[4,128,256]{2,1,0:T(8,128)(2,1)}, bf16[4,128,256]{2,1,0:T(8,128)(2,1)}, u32[]{:S(2)}, u32[]{:S(2)}) collective-permute-start(bf16[4,128,256]{2,1,0:T(8,128)(2,1)} %fusion.590), channel_id=1, source_target_pairs={{4,0},{8,4},{12,8},{5,1},{9,5},{13,9},{6,2},{10,6},{14,10},{7,3},{... | collective-permute-start | bytes 786440 | tf_op jit(solution)/shard_map/while/body/eval_jaxpr/ppermute | solution.py:21
  1328.3 21.4 %collective-permute-start.3 = (f32[3,2048]{1,0:T(4,128)S(1)}, f32[3,2048]{1,0:T(4,128)S(1)}, u32[]{:S(2)}, u32[]{:S(2)}) collective-permute-start(f32[3,2048]{1,0:T(4,128)S(1)} %pad_add_fusion.7), channel_id=1, source_target_pairs={{4,0},{8,4},{12,8},{5,1},{9,5},{13,9},{6,2},{10,6},{14,10},{7,3},{... | collective-permute-start | bytes 73736 | tf_op jit(solution)/shard_map/ppermute | solution.py:21
  1352.6 13.4 all-to-all-start.12
  1369.6 230.0 %reduce-scatter.2.cloned.1.call-start = ((), (), s32[]{:S(2)}) async-start(), calls=%async_computation.24 | async-start | bytes 18382848 | tf_op jit(solution)/shard_map/reduce_scatter | solution.py:426
  1434.9 67.6 %all-to-all-start.8 = ((bf16[2,128,512]{1,2,0:T(8,128)(2,1)}), bf16[2,128,512]{1,2,0:T(8,128)(2,1)S(1)}, u32[]{:S(2)}, u32[]{:S(2)}) async-start(bf16[2,128,512]{1,2,0:T(8,128)(2,1)} %copy.489), calls=%async_computation.8 | async-start | bytes 524288 | tf_op jit(solution)/shard_map/all_to_all | solution.py:401
  (240 other events, 3108.4 us)
Sparse Core Ops, SparseCore 0:
  10.9 59.0 all-gather.10
  72.8 56.7 all-gather.12
  132.5 60.7 all-gather.14
  196.0 61.0 all-gather.16
  259.7 60.9 all-gather.18
  323.5 67.5 all-gather.20
  394.1 66.8 all-gather.22
  463.9 68.1 all-gather.24
  1414.3 185.2 reduce-scatter.1
where the time goes:
time: 1630 us; the launch traced here: 1610 us
  other arithmetic  479 us (29%)
  matrix products  337 us (21%)
  local copies, waits for them, and re-layouts  261 us (16%)
  blocking collectives  221 us (14%)
  waiting for transfers between devices  217 us (13%)
  starting transfers between devices  78.1 us (5%)
    another operation x72, other arithmetic, span_parts(): jax.scipy.linalg.solve_triangular(system, targets, lower=True, unit_diago...  349 us
    unnamed x2, blocking collectives  80 us
    ppermute x8, waiting for transfers between devices, passed_along(): return lax.ppermute(block, axis, route)  64.3 us
    psum x1, blocking collectives, body(): lax.psum((conv_grad[:, :query_width], conv_grad[:, query_width:2 * query_...  62.4 us
    another operation x57, local copies, waits for them, and re-layouts  54.4 us
    all_gather x1, waiting for transfers between devices, body(): lax.all_gather(w_value, ('head', 'ctx', 'batch'), axis=0, tiled=True)  52.8 us
    all_gather x1, waiting for transfers between devices, body(): lax.all_gather(w_gate, ('head', 'ctx', 'batch'), axis=0, tiled=True)  42.9 us
    another operation x24, matrix products, span_parts(): jax.scipy.linalg.solve_triangular(system, targets, lower=True, unit_diago...  42.8 us
  transfers between devices with their start and end apart: 32, of which 15 were waited for; matrix products, arithmetic and copies ran while one was open for 62% of the time, Pallas kernels for 0%

commit v1 on v0

v1 whole, which is shorter than its diff:
```python
import math

import jax
import jax.numpy as jnp
from jax import lax
from jax.experimental import pallas as pl
from jax.experimental.pallas import tpu as pltpu
from jax.sharding import PartitionSpec as P

KW = 4
CHUNK = 256
epsilon = 1e-06
highest_precision = lax.Precision.HIGHEST


def passed_along(block, axis, distance):
    devices = range(lax.axis_size(axis))
    route = [(i - distance, i) for i in devices if i - distance in devices]
    return lax.ppermute(block, axis, route)


def product(first, second, first_dim, second_dim):
    return lax.dot_general(
        first,
        second,
        (((first_dim,), (second_dim,)), ((), ())),
        precision=highest_precision,
        preferred_element_type=jnp.float32,
    )


@jax.custom_vjp
def mul_nn(first, second):
    return product(first, second, 1, 0)


@jax.custom_vjp
def mul_nt(first, second):
    return product(first, second, 1, 1)


@jax.custom_vjp
def mul_tn(first, second):
    return product(first, second, 0, 0)


mul_nn.defvjp(
    lambda a, b: (product(a, b, 1, 0), (a, b)),
    lambda res, ct: (product(ct, res[1], 1, 1), product(res[0], ct, 0, 0)),
)
mul_nt.defvjp(
    lambda a, b: (product(a, b, 1, 1), (a, b)),
    lambda res, ct: (product(ct, res[1], 1, 0), product(ct, res[0], 0, 0)),
)
mul_tn.defvjp(
    lambda a, b: (product(a, b, 0, 0), (a, b)),
    lambda res, ct: (product(res[1], ct, 1, 1), product(res[0], ct, 1, 0)),
)


@jax.custom_vjp
def solve_with(inverse, lower, rhs):
    return product(inverse, rhs, 1, 0)


def solve_forward(inverse, lower, rhs):
    solved = product(inverse, rhs, 1, 0)
    return solved, (inverse, solved)


def solve_backward(res, ct):
    inverse, solved = res
    rhs_grad = product(inverse, ct, 0, 0)
    return jnp.zeros_like(inverse), -product(rhs_grad, solved, 1, 1), rhs_grad


solve_with.defvjp(solve_forward, solve_backward)


def square_masks(size):
    rows = lax.broadcasted_iota(jnp.int32, (size, size), 0)
    cols = lax.broadcasted_iota(jnp.int32, (size, size), 1)
    return rows, cols


def unit_lower_inverse(lower):
    size = lower.shape[0]
    rows, cols = square_masks(size)
    inverse = jnp.where(rows == cols, 1.0, 0.0).astype(jnp.float32)
    level = 0
    while (1 << level) < size:
        width = 1 << level
        joined = (rows // (2 * width)) == (cols // (2 * width))
        mask = joined & ((rows // width) > (cols // width))
        off = jnp.where(mask, lower, 0.0)
        if level == 0:
            inverse = inverse - off
        else:
            inverse = inverse - product(product(inverse, off, 1, 0), inverse, 1, 0)
        level += 1
    return inverse


def silu_rows(x):
    return x * lax.logistic(x)


def unit_rows(matrix):
    return matrix * lax.rsqrt(jnp.sum(matrix * matrix, axis=1, keepdims=True) + epsilon)


def piece_terms(query_in, key_in, value_in, decay, strength, nn, nt):
    size = query_in.shape[0]
    width = query_in.shape[1]
    rows, cols = square_masks(size)
    strict = rows > cols
    inclusive = rows >= cols
    ones_low = jnp.where(inclusive, 1.0, 0.0).astype(jnp.float32)
    ones_high = jnp.where(rows < cols, 1.0, 0.0).astype(jnp.float32)
    queries = unit_rows(silu_rows(query_in)) * (1.0 / math.sqrt(width))
    keys = unit_rows(silu_rows(key_in))
    values = silu_rows(value_in)
    gaps = nn(ones_low, jnp.where(strict, jnp.broadcast_to(decay, (size, size)), 0.0))
    spread = jnp.exp(gaps)
    decay_wide = jnp.broadcast_to(decay, (size, width))
    head_decay = jnp.exp(nn(ones_low, decay_wide))
    tail_decay = jnp.exp(nn(ones_high, decay_wide))
    final = jnp.exp(jnp.sum(decay, axis=0, keepdims=True))
    lower = jnp.where(strict, spread * nt(keys, keys), 0.0) * strength
    scores = jnp.where(inclusive, spread * nt(queries, keys), 0.0)
    return (
        lower,
        scores,
        head_decay * queries,
        head_decay * keys,
        tail_decay * keys,
        values,
        final,
    )


def plain_nn(a, b):
    return product(a, b, 1, 0)


def plain_nt(a, b):
    return product(a, b, 1, 1)


def forward_kernel(q_ref, k_ref, v_ref, d_ref, s_ref, x_ref, o_ref, e_ref, m_ref, f_ref):
    strength = s_ref[...]
    lower, scores, led_queries, led_keys, tail_keys, values, final = piece_terms(
        q_ref[...], k_ref[...], v_ref[...], d_ref[...], strength, plain_nn, plain_nt
    )
    inverse = unit_lower_inverse(lower)
    x_ref[...] = inverse
    direct = product(inverse, strength * values, 1, 0)
    across = product(inverse, strength * led_keys, 1, 0)
    o_ref[...] = product(scores, direct, 1, 0)
    e_ref[...] = led_queries - product(scores, across, 1, 0)
    width = led_keys.shape[1]
    rows, cols = square_masks(width)
    m_ref[...] = jnp.where(rows == cols, jnp.broadcast_to(final, (width, width)), 0.0) - product(
        tail_keys, across, 0, 0
    )
    f_ref[...] = product(tail_keys, direct, 0, 0)


def backward_kernel(
    q_ref, k_ref, v_ref, d_ref, s_ref, x_ref, i_ref, g_ref, t_ref,
    dq_ref, dk_ref, dv_ref, dd_ref, ds_ref,
):
    inverse = x_ref[...]
    start = i_ref[...]

    def run(query_in, key_in, value_in, decay, strength):
        lower, scores, led_queries, led_keys, tail_keys, values, final = piece_terms(
            query_in, key_in, value_in, decay, strength, mul_nn, mul_nt
        )
        update = solve_with(inverse, lower, strength * (values - mul_nn(led_keys, start)))
        mixed = mul_nn(led_queries, start) + mul_nn(scores, update)
        last = final * start + mul_tn(tail_keys, update)
        return mixed, last

    unused, pull = jax.vjp(run, q_ref[...], k_ref[...], v_ref[...], d_ref[...], s_ref[...])
    grads = pull((g_ref[...], t_ref[...]))
    for ref, grad in zip((dq_ref, dk_ref, dv_ref, dd_ref, ds_ref), grads):
        ref[...] = grad


def out_gate(mixer_rows, gate_rows, gain_row):
    scale = lax.rsqrt(jnp.mean(mixer_rows * mixer_rows, axis=1, keepdims=True) + epsilon)
    return mixer_rows * scale * gain_row * silu_rows(gate_rows)


def gate_kernel(o_ref, e_ref, i_ref, gate_ref, gain_ref, out_ref):
    mixer_rows = o_ref[...] + product(e_ref[...], i_ref[...], 1, 0)
    gated = out_gate(mixer_rows, gate_ref[...].astype(jnp.float32), gain_ref[...])
    out_ref[...] = gated.astype(out_ref.dtype)


def gate_back_kernel(
    o_ref, e_ref, i_ref, gate_ref, gain_ref, grad_ref, mg_ref, gg_ref, ng_ref, r_ref
):
    effect = e_ref[...]
    mixer_rows = o_ref[...] + product(effect, i_ref[...], 1, 0)
    unused, pull = jax.vjp(
        out_gate, mixer_rows, gate_ref[...].astype(jnp.float32), gain_ref[...]
    )
    mixer_grad, gate_grad, gain_grad = pull(grad_ref[...].astype(jnp.float32))
    mg_ref[...] = mixer_grad
    gg_ref[...] = gate_grad.astype(gg_ref.dtype)
    ng_ref[...] = gain_grad
    r_ref[...] = product(effect, mixer_grad, 0, 0)


def per_head(kernel, grid, ins, outs, args, flops):
    return pl.pallas_call(
        kernel,
        grid=grid,
        in_specs=ins,
        out_specs=[spec for spec, _ in outs],
        out_shape=[shape for _, shape in outs],
        cost_estimate=pl.CostEstimate(
            flops=flops, bytes_accessed=sum(a.size * a.dtype.itemsize for a in args), transcendentals=0
        ),
    )(*args)


def columns(rows, width, first):
    return pl.BlockSpec((rows, width), lambda h, c, first=first: (c, first + h))


def heads_spec(*shape):
    return pl.BlockSpec((None, None) + shape, lambda h, c: (h, c) + (0,) * len(shape))


def of_shape(shape, kind=jnp.float32):
    return jax.ShapeDtypeStruct(shape, kind)


def state_product(state_map, held):
    return jnp.einsum("hij,hjv->hiv", state_map, held, precision=highest_precision)


def state_pull(state_map, held):
    return jnp.einsum("hji,hjv->hiv", state_map, held, precision=highest_precision)


def mat_nt(first_mat, second_mat):
    return lax.dot_general(
        first_mat, second_mat, (((1,), (1,)), ((), ())), preferred_element_type=jnp.float32
    )


def mat_tn(first_mat, second_mat):
    return lax.dot_general(
        first_mat, second_mat, (((0,), (0,)), ((), ())), preferred_element_type=jnp.float32
    )


def mat_nn(first_mat, second_mat):
    return jnp.dot(first_mat, second_mat, preferred_element_type=jnp.float32)


def rms_scale(hidden, gain_vec):
    return (
        hidden * lax.rsqrt(jnp.mean(hidden * hidden, axis=-1, keepdims=True) + epsilon) * gain_vec
    )


def swiglu(gate_part, up_part):
    return jax.nn.silu(gate_part) * up_part


def short_conv(padded, conv_all):
    length = padded.shape[0] - (KW - 1)
    mixed_rows = padded[0:length] * conv_all[0]
    for tap_index in range(1, KW):
        mixed_rows = mixed_rows + padded[tap_index : tap_index + length] * conv_all[tap_index]
    return mixed_rows


def decay_rates(rates, decay_log, decay_bias):
    heads = decay_log.shape[0]
    pairs = jnp.transpose(rates.reshape(rates.shape[0], heads, 2), (2, 1, 0))
    log_decay = -jnp.exp(decay_log)[:, None] * jax.nn.softplus(pairs[0] + decay_bias[:, None])
    strength = jax.nn.sigmoid(pairs[1])
    return log_decay[:, :, None], strength[:, :, None]


def split_columns(matrix, widths):
    pieces = []
    offset_col = 0
    for width_one in widths:
        pieces.append(matrix[:, offset_col : offset_col + width_one])
        offset_col = offset_col + width_one
    return pieces


def head_halves(weights, parts):
    slabs = []
    for part in range(parts):
        cut = []
        for weight in weights:
            width = weight.shape[1] // parts
            cut.append(weight[:, part * width : (part + 1) * width])
        slabs.append(jnp.concatenate(cut, axis=1))
    return jnp.stack(slabs)


def swap_halves(slabs):
    return lax.all_to_all(slabs, "head", split_axis=0, concat_axis=0, tiled=True)


def whole_rows(slabs):
    full = lax.all_gather(slabs, ("ctx", "batch"), axis=1, tiled=True)
    return full.reshape(full.shape[0] * full.shape[1], full.shape[2])


def other_parts(block):
    parts = lax.axis_size("head")
    total = None
    for shift in range(1, parts):
        moved = lax.ppermute(block, "head", [(i, (i + shift) % parts) for i in range(parts)])
        moved = moved.astype(jnp.float32)
        total = moved if total is None else total + moved
    return total


def head_sum(partial, kind=jnp.bfloat16):
    sent = partial.astype(kind)
    if lax.axis_size("head") == 1:
        return sent.astype(jnp.float32)
    return sent.astype(jnp.float32) + other_parts(sent)


def own_rows_sum(partial):
    parts = lax.axis_size("head")
    rows = partial.shape[0] // parts
    me = lax.axis_index("head")
    total = lax.dynamic_slice_in_dim(partial, me * rows, rows, 0)
    for shift in range(1, parts):
        target = lax.rem(me + shift, parts)
        sent = lax.dynamic_slice_in_dim(partial, target * rows, rows, 0).astype(jnp.bfloat16)
        route = [(i, (i + shift) % parts) for i in range(parts)]
        total = total + lax.ppermute(sent, "head", route).astype(jnp.float32)
    return total


def body(
    tokens,
    cotangent,
    norm1_gain,
    w_query,
    w_key,
    w_value,
    w_gate,
    w_rates,
    conv_query,
    conv_key,
    conv_value,
    decay_log,
    decay_bias,
    out_gain,
    w_out,
    norm2_gain,
    w_ffgate,
    w_ffup,
    w_down,
):
    parts = lax.axis_size("head")
    me = lax.axis_index("head")
    heads = decay_log.shape[0]
    query_width = conv_query.shape[1]
    value_width = conv_value.shape[1]
    dk = query_width // heads
    dv = value_width // heads
    margin = KW - 1
    gains = jnp.stack([norm1_gain, norm2_gain], axis=1)
    slabs_in = head_halves(
        [w_query, w_key, w_value, w_gate, w_rates, jnp.tile(gains, (1, parts))], parts
    )
    in_weight = whole_rows(swap_halves(slabs_in))
    rates_width = w_rates.shape[1] // parts
    mixed_width = 2 * query_width + value_width
    proj_width = mixed_width + value_width + rates_width
    gain_cols = in_weight[:, proj_width:].astype(jnp.float32)
    gain_one = gain_cols[:, 0]
    gain_two = gain_cols[:, 1]
    later = swap_halves(head_halves([w_out, w_ffgate, w_ffup, w_down], parts))
    ff_local = w_down.shape[1] // parts
    out_weight = whole_rows(later[:, :, :value_width])
    ff_weight = whole_rows(later[:, :, value_width : value_width + 2 * ff_local])
    down_weight = whole_rows(later[:, :, value_width + 2 * ff_local :])

    inputs_tok = tokens[0]
    own_count = inputs_tok.shape[0]
    piece_tok = lax.all_gather(inputs_tok, "head", axis=0, tiled=True)
    cot = lax.all_gather(cotangent[0], "head", axis=0, tiled=True)
    residual = piece_tok.astype(jnp.float32)
    piece_rows = residual.shape[0]
    normed_one = rms_scale(residual, gain_one).astype(jnp.bfloat16)
    proj = mat_nn(normed_one, in_weight[:, :proj_width]).astype(jnp.bfloat16)
    joined = proj[:, :mixed_width]
    rates_here = proj[:, mixed_width + value_width :]
    rim_rows = passed_along(joined[piece_rows - margin :], "ctx", 1)
    padded = jnp.concatenate([rim_rows, joined], axis=0).astype(jnp.float32)
    conv_all = jnp.concatenate([conv_query, conv_key, conv_value], axis=1).astype(jnp.float32)
    mixed, conv_vjp = jax.vjp(short_conv, padded, conv_all)
    (log_decay, strength), rates_vjp = jax.vjp(
        decay_rates, rates_here.astype(jnp.float32), decay_log, decay_bias
    )
    value_first = 2 * query_width // dv
    chunk = min(CHUNK, piece_rows)
    chunks = piece_rows // chunk
    grid = (heads, chunks)
    log_decay = log_decay.reshape(heads, chunks, chunk, 1)
    strength = strength.reshape(heads, chunks, chunk, 1)
    mixed_specs = [
        columns(chunk, dk, 0),
        columns(chunk, dk, heads),
        columns(chunk, dv, value_first),
        heads_spec(chunk, 1),
        heads_spec(chunk, 1),
    ]
    square = heads_spec(chunk, chunk)
    state = heads_spec(dk, dv)
    rows_v = columns(chunk, dv, 0)
    rows_k = columns(chunk, dk, 0)
    inverse, local_out, effect, state_map, state_offset = per_head(
        forward_kernel,
        grid,
        mixed_specs,
        [
            (square, of_shape((heads, chunks, chunk, chunk))),
            (rows_v, of_shape((piece_rows, value_width))),
            (rows_k, of_shape((piece_rows, query_width))),
            (heads_spec(dk, dk), of_shape((heads, chunks, dk, dk))),
            (state, of_shape((heads, chunks, dk, dv))),
        ],
        (mixed, mixed, mixed, log_decay, strength),
        heads * 100 * piece_rows * chunk**2,
    )
    chunk_maps = [state_map[:, i] for i in range(chunks)]
    chunk_offsets = [state_offset[:, i] for i in range(chunks)]
    piece_map = chunk_maps[0]
    piece_offset = chunk_offsets[0]
    for i in range(1, chunks):
        piece_map = state_product(chunk_maps[i], piece_map)
        piece_offset = state_product(chunk_maps[i], piece_offset) + chunk_offsets[i]
    last_step = lax.axis_size("ctx") - 1
    start_state = jnp.zeros_like(piece_offset)
    for step in range(last_step):
        moved = piece_offset
        if step > 0:
            moved = moved + state_product(piece_map, start_state)
        start_state = passed_along(moved.astype(jnp.bfloat16), "ctx", 1).astype(jnp.float32)
    starts = [start_state]
    for i in range(1, chunks):
        starts.append(state_product(chunk_maps[i - 1], starts[-1]) + chunk_offsets[i - 1])
    start_states = jnp.stack(starts, axis=1)
    gain_row = out_gain.astype(jnp.float32)[None]
    gate_spec = columns(chunk, dv, mixed_width // dv)
    gain_spec = pl.BlockSpec((1, dv), lambda h, c: (0, h))
    gain_out = pl.BlockSpec((None, 1, dv), lambda h, c: (c, 0, h))
    gate_ins = [rows_v, rows_k, state, gate_spec, gain_spec]
    gate_args = (local_out, effect, start_states, proj, gain_row)
    (gated,) = per_head(
        gate_kernel,
        grid,
        gate_ins,
        [(rows_v, of_shape((piece_rows, value_width), jnp.bfloat16))],
        gate_args,
        heads * 12 * piece_rows * dk * dv,
    )
    middle = residual + head_sum(mat_nt(gated, out_weight))
    normed_two_f, norm_two_vjp = jax.vjp(rms_scale, middle, gain_two)
    normed_two = normed_two_f.astype(jnp.bfloat16)
    ff_both = mat_nn(normed_two, ff_weight)
    hidden_f, swiglu_vjp = jax.vjp(swiglu, ff_both[:, :ff_local], ff_both[:, ff_local:])
    hidden = hidden_f.astype(jnp.bfloat16)
    hidden_grad = mat_nn(cot, down_weight)
    gate_grad_f, up_grad_f = swiglu_vjp(hidden_grad)
    ff_grads = jnp.concatenate([gate_grad_f, up_grad_f], axis=1).astype(jnp.bfloat16)
    middle_part, gain_two_grad = norm_two_vjp(head_sum(mat_nt(ff_grads, ff_weight)))
    middle_grad = cot.astype(jnp.float32) + middle_part
    middle_grad_b = middle_grad.astype(jnp.bfloat16)
    gated_grad = mat_nn(middle_grad_b, out_weight).astype(jnp.bfloat16)
    middle_own = lax.dynamic_slice_in_dim(middle, me * own_count, own_count, 0)
    output_tok = (middle_own + own_rows_sum(mat_nt(hidden, down_weight))).astype(jnp.bfloat16)

    mixer_grad, gate_bf, out_gain_grad, reach = per_head(
        gate_back_kernel,
        grid,
        gate_ins + [rows_v],
        [
            (rows_v, of_shape((piece_rows, value_width))),
            (rows_v, of_shape((piece_rows, value_width), jnp.bfloat16)),
            (gain_out, of_shape((chunks, 1, value_width))),
            (state, of_shape((heads, chunks, dk, dv))),
        ],
        gate_args + (gated_grad,),
        heads * 24 * piece_rows * dk * dv,
    )
    chunk_reach = [reach[:, i] for i in range(chunks)]
    piece_reach = chunk_reach[chunks - 1]
    for i in range(chunks - 2, -1, -1):
        piece_reach = chunk_reach[i] + state_pull(chunk_maps[i], piece_reach)
    last_grad = jnp.zeros_like(piece_reach)
    for step in range(last_step):
        moved = piece_reach
        if step > 0:
            moved = moved + state_pull(piece_map, last_grad)
        last_grad = passed_along(moved.astype(jnp.bfloat16), "ctx", -1).astype(jnp.float32)
    lasts = [last_grad]
    for i in range(chunks - 1, 0, -1):
        lasts.insert(0, chunk_reach[i] + state_pull(chunk_maps[i], lasts[0]))
    last_grads = jnp.stack(lasts, axis=1)

    ff_sums = lax.psum_scatter(
        jnp.concatenate(
            [
                mat_tn(middle_grad_b, gated).astype(jnp.bfloat16),
                mat_tn(normed_two, ff_grads).astype(jnp.bfloat16),
                mat_tn(cot, hidden).astype(jnp.bfloat16),
            ],
            axis=1,
        ),
        ("ctx", "batch"),
        scatter_dimension=0,
        tiled=True,
    ).astype(jnp.float32)
    ff_parts = split_columns(ff_sums, (value_width, ff_local, ff_local, ff_local))

    query_g, key_g, value_g, decay_g, strength_g = per_head(
        backward_kernel,
        grid,
        mixed_specs + [square, state, rows_v, state],
        [
            (rows_k, of_shape((piece_rows, query_width))),
            (rows_k, of_shape((piece_rows, query_width))),
            (rows_v, of_shape((piece_rows, value_width))),
            (heads_spec(chunk, 1), of_shape((heads, chunks, chunk, 1))),
            (heads_spec(chunk, 1), of_shape((heads, chunks, chunk, 1))),
        ],
        (mixed, mixed, mixed, log_decay, strength, inverse, start_states, mixer_grad, last_grads),
        heads * 100 * piece_rows * chunk**2,
    )
    padded_grad, conv_grad = conv_vjp(jnp.concatenate([query_g, key_g, value_g], axis=1))
    rates_grad_f, decay_log_grad, decay_bias_grad = rates_vjp(
        (decay_g.reshape(heads, piece_rows, 1), strength_g.reshape(heads, piece_rows, 1))
    )
    back_rim = passed_along(padded_grad[:margin], "ctx", -1)
    own_rows = padded_grad[margin:]
    own_rows = jnp.concatenate(
        [own_rows[: piece_rows - margin], own_rows[piece_rows - margin :] + back_rim], axis=0
    ).astype(jnp.bfloat16)
    proj_grad = jnp.concatenate([own_rows, gate_bf, rates_grad_f.astype(jnp.bfloat16)], axis=1)
    proj_sums = lax.psum_scatter(
        mat_tn(normed_one, proj_grad).astype(jnp.bfloat16),
        ("ctx", "batch"),
        scatter_dimension=0,
        tiled=True,
    ).astype(jnp.float32)
    proj_parts = split_columns(
        proj_sums, (query_width, query_width, value_width, value_width, rates_width)
    )
    own_grad = own_rows_sum(mat_nt(proj_grad, in_weight[:, :proj_width]))
    unused_rows, norm_one_vjp = jax.vjp(rms_scale, inputs_tok.astype(jnp.float32), gain_one)
    input_part, gain_one_grad = norm_one_vjp(own_grad)
    input_grad = lax.dynamic_slice_in_dim(middle_grad, me * own_count, own_count, 0) + input_part
    smalls = (
        conv_grad.reshape(-1),
        jnp.sum(out_gain_grad, axis=(0, 1)),
        head_sum(gain_one_grad, jnp.float32),
        gain_two_grad,
        decay_log_grad,
        decay_bias_grad,
    )
    summed = lax.psum(jnp.concatenate(smalls), ("ctx", "batch"))
    cuts = []
    first = 0
    for small in smalls:
        cuts.append(summed[first : first + small.shape[0]])
        first += small.shape[0]
    conv_sum = cuts[0].reshape(conv_grad.shape)
    share = norm1_gain.shape[0]
    place = (me * lax.axis_size("ctx") + lax.axis_index("ctx")) * lax.axis_size("batch")
    place = (place + lax.axis_index("batch")) * share
    return (
        output_tok[None],
        input_grad[None],
        lax.dynamic_slice_in_dim(cuts[2], place, share, 0),
        proj_parts[0],
        proj_parts[1],
        proj_parts[2],
        proj_parts[3],
        proj_parts[4],
        conv_sum[:, :query_width],
        conv_sum[:, query_width : 2 * query_width],
        conv_sum[:, 2 * query_width :],
        cuts[4],
        cuts[5],
        cuts[1],
        ff_parts[0],
        lax.dynamic_slice_in_dim(cuts[3], place, share, 0),
        ff_parts[1],
        ff_parts[2],
        ff_parts[3],
    )


def solution(mesh):
    placed = (
        P("batch", ("ctx", "head"), None),
        P("batch", ("ctx", "head"), None),
        P(("head", "ctx", "batch")),
        P(("head", "ctx", "batch"), None),
        P(("head", "ctx", "batch"), None),
        P(("head", "ctx", "batch"), None),
        P(("head", "ctx", "batch"), None),
        P(("head", "ctx", "batch"), None),
        P(None, "head"),
        P(None, "head"),
        P(None, "head"),
        P("head"),
        P("head"),
        P("head"),
        P(("head", "ctx", "batch"), None),
        P(("head", "ctx", "batch")),
        P(("head", "ctx", "batch"), None),
        P(("head", "ctx", "batch"), None),
        P(("head", "ctx", "batch"), None),
    )
    return jax.shard_map(
        body,
        mesh=mesh,
        in_specs=placed,
        out_specs=(
            P("batch", ("ctx", "head"), None),
            P("batch", ("ctx", "head"), None),
            P(("head", "ctx", "batch")),
            P(("ctx", "batch"), "head"),
            P(("ctx", "batch"), "head"),
            P(("ctx", "batch"), "head"),
            P(("ctx", "batch"), "head"),
            P(("ctx", "batch"), "head"),
            P(None, "head"),
            P(None, "head"),
            P(None, "head"),
            P("head"),
            P("head"),
            P("head"),
            P(("ctx", "batch"), "head"),
            P(("head", "ctx", "batch")),
            P(("ctx", "batch"), "head"),
            P(("ctx", "batch"), "head"),
            P(("ctx", "batch"), "head"),
        ),
        check_vma=False,
    )
```

time: 1630 us -> 584 us (0.36)
  other arithmetic: 479 us -> 31.2 us
  matrix products: 337 us -> 47.6 us
  local copies, waits for them, and re-layouts: 261 us -> 35.3 us
  blocking collectives: 221 us -> 100 us
  Pallas kernels: 0 us -> 77.3 us
  starting transfers between devices: 78.1 us -> 35.4 us
  waiting for transfers between devices: 217 us -> 237 us
    another operation x92 -> x7, other arithmetic: 355 us -> 3.48 us  [the longest x72 349 us: span_parts(): jax.scipy.linalg.solve_triangular(system, targets, lower=True, unit_diago...]
    dot_general x156 -> x8, matrix products: 246 us -> 21.3 us  [the longest x4 17.6 us: mat_nn(): return jnp.dot(first_mat, second_mat, preferred_element_type=jnp.float32)]
    unnamed x2 -> x0, blocking collectives: 80 us -> none
    pallas_call x0 -> x4, Pallas kernels: none -> 77.3 us  [per_head(): pl.pallas_call(kernel, grid=grid, in_specs=ins, out_specs=[spec for spec,...]
    reduce_scatter x1 -> x2, waiting for transfers between devices: 27.2 us -> 90 us  [the longest x1 90 us: body(): lax.psum_scatter(jnp.concatenate([mat_tn(middle_grad_b, gated).astype(jnp...]
    all_gather x5 -> x2, blocking collectives: 78.5 us -> 18.1 us  [the longest x1 10.9 us: body(): cot = lax.all_gather(cotangent[0], 'head', axis=0, tiled=True)]
    all_to_all x15 -> x0, starting transfers between devices: 55.9 us -> none  [the longest x1 4.68 us: body(): lax.all_to_all(ffup_grad, 'head', split_axis=1, concat_axis=0, tiled=True)]
    another operation x61 -> x1, local copies, waits for them, and re-layouts: 55.6 us -> 0.01 us  [body(): jnp.tile(gains, (1, parts))]
  transfers between devices with their start and end apart: 32 -> 19, of which waited for: 15 -> 14; matrix products, arithmetic and copies ran while one was open for 62% -> 12% of each run, Pallas kernels for 0% -> 8%
where the time goes in v1:
time: 584 us; the launch traced here: 579 us
  waiting for transfers between devices  237 us (41%)
  blocking collectives  100 us (17%)
  Pallas kernels  77.3 us (13%)
  matrix products  47.6 us (8%)
  starting transfers between devices  35.4 us (6%)
  local copies, waits for them, and re-layouts  35.3 us (6%)
  other arithmetic  31.2 us (5%)
  between operations  15.3 us (3%)
    reduce_scatter x1, waiting for transfers between devices, body(): lax.psum_scatter(jnp.concatenate([mat_tn(middle_grad_b, gated).astype(jnp...  90 us
    pallas_call x4, Pallas kernels, per_head(): pl.pallas_call(kernel, grid=grid, in_specs=ins, out_specs=[spec for spec,...  77.3 us
    all_gather x4, waiting for transfers between devices, whole_rows(): full = lax.all_gather(slabs, ('ctx', 'batch'), axis=1, tiled=True)  67.4 us
    psum x1, blocking collectives, body(): summed = lax.psum(jnp.concatenate(smalls), ('ctx', 'batch'))  58.9 us
    ppermute x8, waiting for transfers between devices, passed_along(): return lax.ppermute(block, axis, route)  56.6 us
    ppermute x8, starting transfers between devices, passed_along(): return lax.ppermute(block, axis, route)  25.5 us
    all_to_all x2, blocking collectives, swap_halves(): lax.all_to_all(slabs, 'head', split_axis=0, concat_axis=0, tiled=True)  23.1 us
    dot_general x4, matrix products, mat_nn(): return jnp.dot(first_mat, second_mat, preferred_element_type=jnp.float32)  17.6 us
  transfers between devices with their start and end apart: 19, of which 14 were waited for; matrix products, arithmetic and copies ran while one was open for 12% of the time, Pallas kernels for 8%

profile of v1, /device:TPU:0, one launch (start us, length us, event | category | flops | bytes accessed | tf_op | source)
XLA Modules:
  0.0 579.2 jit_solution(4192450264372149829)
XLA Ops:
  11.2 11.4 %all_to_all.10 = bf16[2,32,3082]{2,1,0:T(8,128)(2,1)} all-to-all(bf16[2,32,3082]{2,1,0:T(8,128)(2,1)S(1)} %pad_maximum_fusion.6), channel_id=1, replica_groups=mesh['head'=2,'ctx'=4,'batch'=4] {'head'}, dimensions={0} | all-to-all | bytes 788992 | tf_op jit(solution)/shard_map/all_to_all | solution.py:313
  23.1 11.7 %all_to_all.11 = bf16[2,32,5248]{2,1,0:T(8,128)(2,1)S(1)} all-to-all(bf16[2,32,5248]{2,1,0:T(8,128)(2,1)S(1)} %pad_maximum_fusion.5), channel_id=1, replica_groups=mesh['head'=2,'ctx'=4,'batch'=4] {'head'}, dimensions={0} | all-to-all | bytes 1343488 | tf_op jit(solution)/shard_map/all_to_all | solution.py:313
  36.3 7.2 %all-gather = bf16[1,256,1024]{2,1,0:T(8,128)(2,1)S(1)} all-gather(bf16[1,128,1024]{2,1,0:T(8,128)(2,1)S(1)} %copy-done.16), channel_id=2, replica_groups=mesh['head'=2,'ctx'=4,'batch'=4] {'head'}, dimensions={1}, use_global_device_ids=true | all-gather | bytes 786432 | tf_op jit(solution)/shard_map/all_gather | solution.py:399
  44.6 41.6 %all-gather.7.cloned.1.call-done = bf16[2,512,3082]{2,1,0:T(8,128)(2,1)} async-done(((bf16[2,32,3082]{2,1,0:T(8,128)(2,1)}), bf16[2,512,3082]{2,1,0:T(8,128)(2,1)}) %all-gather.7.cloned.1.call-update) | async-done | bytes 6311952 | tf_op jit(solution)/shard_map/all_gather | solution.py:317
  87.5 4.9 fusion.4.gate_ref
  101.6 39.0 %shard_map.330 = (f32[4,1,256,256]{3,2,1,0:T(8,128)}, f32[256,1024]{1,0:T(8,128)}, f32[256,512]{1,0:T(8,128)}, f32[4,1,128,128]{3,2,1,0:T(8,128)}, f32[4,1,128,256]{3,2,1,0:T(8,128)}) custom-call(f32[256,2048]{1,0:T(8,128)} %multiply_add_fusion.q_ref.k_ref.v_ref, f32[256,2048]{1,0:T(8,128)} %multiply_add_fusion.q_ref.k_ref.v_ref, ...), custom_call_target="tpu_custom_call" | custom-call | flops 6710886400 | bytes 6299648 | tf_op jit(solution)/shard_map/pallas_call | solution.py:218
  144.7 11.6 %collective-permute-done.1 = bf16[4,128,256]{2,1,0:T(8,128)(2,1)S(1)} collective-permute-done((bf16[4,128,256]{2,1,0:T(8,128)(2,1)S(1)}, bf16[4,128,256]{2,1,0:T(8,128)(2,1)S(1)}, u32[]{:S(2)}, u32[]{:S(2)}) %collective-permute-start.1) | collective-permute-done | bytes 262176 | tf_op jit(solution)/shard_map/ppermute | solution.py:19
  162.2 10.6 %collective-permute-done.2 = bf16[4,128,256]{2,1,0:T(8,128)(2,1)S(1)} collective-permute-done((bf16[4,128,256]{2,1,0:T(8,128)(2,1)S(1)}, bf16[4,128,256]{2,1,0:T(8,128)(2,1)S(1)}, u32[]{:S(2)}, u32[]{:S(2)}) %collective-permute-start.2) | collective-permute-done | bytes 262176 | tf_op jit(solution)/shard_map/ppermute | solution.py:19
  173.3 8.8 %collective-permute-start.3 = (bf16[4,128,256]{2,1,0:T(8,128)(2,1)S(1)}, bf16[4,128,256]{2,1,0:T(8,128)(2,1)S(1)}, u32[]{:S(2)}, u32[]{:S(2)}) collective-permute-start(bf16[4,128,256]{2,1,0:T(8,128)(2,1)S(1)} %fusion.13), channel_id=1, source_target_pairs={{0,4},{4,8},{8,12},{1,5},{5,9},{9,13},{2,6},{6,10},{10,14},{3,7},{... | collective-permute-start | bytes 786440 | tf_op jit(solution)/shard_map/ppermute | solution.py:19
  182.6 9.4 %collective-permute-done.3 = bf16[4,128,256]{2,1,0:T(8,128)(2,1)S(1)} collective-permute-done((bf16[4,128,256]{2,1,0:T(8,128)(2,1)S(1)}, bf16[4,128,256]{2,1,0:T(8,128)(2,1)S(1)}, u32[]{:S(2)}, u32[]{:S(2)}) %collective-permute-start.3) | collective-permute-done | bytes 262176 | tf_op jit(solution)/shard_map/ppermute | solution.py:19
  202.8 10.9 %all-gather.1 = bf16[1,256,1024]{2,1,0:T(8,128)(2,1)} all-gather(bf16[1,128,1024]{2,1,0:T(8,128)(2,1)S(1)} %copy-done.28), channel_id=3, replica_groups=mesh['head'=2,'ctx'=4,'batch'=4] {'head'}, dimensions={1}, use_global_device_ids=true | all-gather | bytes 786432 | tf_op jit(solution)/shard_map/all_gather | solution.py:400
  214.2 6.0 %fusion.59 = f32[256,2816]{1,0:T(8,128)} fusion(bf16[1024,2816]{1,0:T(8,128)(2,1)} %bitcast.159, f32[256,1024]{1,0:T(8,128)S(1)} %get-tuple-element.134, f32[1024]{0:T(1024)S(1)} %bitcast.128, f32[256]{0:T(256)S(1)} %fusion.52), kind=kOutput, calls=%fused_computation.143 | convolution fusion | flops 1477181440 | bytes 9704448 | tf_op jit(solution)/shard_map/dot_general | solution.py:263
  220.2 25.8 %all-gather.13.cloned.1.call-done = bf16[2,512,1408]{2,1,0:T(8,128)(2,1)} async-done(((bf16[2,32,1408]{2,1,0:T(8,128)(2,1)}), bf16[2,512,1408]{2,1,0:T(8,128)(2,1)}) %all-gather.13.cloned.1.call-update) | async-done | bytes 2883600 | tf_op jit(solution)/shard_map/all_gather | solution.py:317
  245.9 5.2 fusion.10
  254.4 12.6 %collective-permute-done.6 = bf16[256,1024]{1,0:T(8,128)(2,1)S(1)} collective-permute-done((bf16[256,1024]{1,0:T(8,128)(2,1)S(1)}, bf16[256,1024]{1,0:T(8,128)(2,1)S(1)}, u32[]{:S(2)}, u32[]{:S(2)}) %collective-permute-start.6) | collective-permute-done | bytes 524320 | tf_op jit(solution)/shard_map/ppermute | solution.py:325
  270.8 6.1 %shard_map.332 = (f32[256,1024]{1,0:T(8,128)}, bf16[256,1024]{1,0:T(8,128)(2,1)}, f32[1,1,1024]{2,1,0:T(1,128)}, f32[4,1,128,256]{3,2,1,0:T(8,128)}) custom-call(f32[256,1024]{1,0:T(8,128)} %get-tuple-element.33.o_ref, f32[256,512]{1,0:T(8,128)} %get-tuple-element.34.e_ref, f32[4,1,128,256]{3,2,1,0:T(8,128)} %bitcast_convert_fusion.3.i_ref, ...), custom_call_target="tpu_custom_call" | custom-call | flops 805306368 | bytes 4202496 | tf_op jit(solution)/shard_map/pallas_call | solution.py:218
  279.4 8.2 %collective-permute-done.7 = bf16[4,128,256]{2,1,0:T(8,128)(2,1)S(1)} collective-permute-done((bf16[4,128,256]{2,1,0:T(8,128)(2,1)S(1)}, bf16[4,128,256]{2,1,0:T(8,128)(2,1)S(1)}, u32[]{:S(2)}, u32[]{:S(2)}) %collective-permute-start.7) | collective-permute-done | bytes 262176 | tf_op jit(solution)/shard_map/ppermute | solution.py:19
  290.4 7.3 %collective-permute-done.8 = bf16[4,128,256]{2,1,0:T(8,128)(2,1)S(1)} collective-permute-done((bf16[4,128,256]{2,1,0:T(8,128)(2,1)S(1)}, bf16[4,128,256]{2,1,0:T(8,128)(2,1)S(1)}, u32[]{:S(2)}, u32[]{:S(2)}) %collective-permute-start.8) | collective-permute-done | bytes 262176 | tf_op jit(solution)/shard_map/ppermute | solution.py:19
  299.6 6.8 %collective-permute-done.9 = bf16[4,128,256]{2,1,0:T(8,128)(2,1)S(1)} collective-permute-done((bf16[4,128,256]{2,1,0:T(8,128)(2,1)S(1)}, bf16[4,128,256]{2,1,0:T(8,128)(2,1)S(1)}, u32[]{:S(2)}, u32[]{:S(2)}) %collective-permute-start.9) | collective-permute-done | bytes 262176 | tf_op jit(solution)/shard_map/ppermute | solution.py:19
  307.2 27.6 %shard_map.333 = (f32[256,512]{1,0:T(8,128)}, f32[256,512]{1,0:T(8,128)}, f32[256,1024]{1,0:T(8,128)}, f32[4,1,256,1]{3,2,1,0:T(8,128)}, f32[4,1,256,1]{3,2,1,0:T(8,128)}) custom-call(f32[256,2048]{1,0:T(8,128)} %multiply_add_fusion.q_ref.k_ref.v_ref, f32[256,2048]{1,0:T(8,128)} %multiply_add_fusion.q_ref.k_ref.v_ref, ...), custom_call_target="tpu_custom_call" | custom-call | flops 6710886400 | bytes 9445376 | tf_op jit(solution)/shard_map/pallas_call | solution.py:218
  372.7 10.0 %pad_maximum_fusion = bf16[1024,5248]{1,0:T(8,128)(2,1)} fusion(bf16[1024,1408]{1,0:T(8,128)(2,1)} %fusion.7, bf16[1024,2816]{1,0:T(8,128)(2,1)} %convolution_convert_fusion.1, bf16[1024,1024]{1,0:T(8,128)(2,1)} %copy.104), kind=kLoop, calls=%fused_computation | loop fusion | flops 32243712 | bytes 21495808 | tf_op jit(solution)/shard_map/concatenate | solution.py:522
  395.2 5.3 fusion
  411.1 58.9 %psum.7 = f32[11272]{0:T(1024)S(1)} all-reduce(f32[11272]{0:T(1024)S(1)} %concatenate.48), channel_id=1, replica_groups=mesh['head'=2,'ctx'=4,'batch'=4] {'ctx','batch'}, use_global_device_ids=true, to_apply=%region_13.14 | all-reduce | flops 11272 | bytes 90176 | tf_op jit(solution)/shard_map/psum | solution.py:581
  478.4 90.0 %reduce-scatter.5.cloned.1.call-done = bf16[64,5248]{1,0:T(8,128)(2,1)} async-done(((bf16[1024,5248]{1,0:T(8,128)(2,1)}), bf16[64,5248]{1,0:T(8,128)(2,1)}) %reduce-scatter.5.cloned.1.call-update) | async-done | bytes 671760 | tf_op jit(solution)/shard_map/reduce_scatter | solution.py:521
  (226 shorter events, 126.9 us)
Async XLA Ops:
  7.2 79.0 %all-gather.7.cloned.1.call-start = ((), (), s32[]{:S(2)}) async-start(), calls=%async_computation.4 | async-start | bytes 6963200 | tf_op jit(solution)/shard_map/all_gather | solution.py:317
  22.7 174.7 %all-gather.9.cloned.1.call-start = ((), (), s32[]{:S(2)}) async-start(), calls=%async_computation.5 | async-start | bytes 2228224 | tf_op jit(solution)/shard_map/all_gather | solution.py:317
  23.0 20.8 %copy-start.33 = (bf16[4,1024]{1,0:T(4,128)(2,1)S(1)}, bf16[4,1024]{1,0:T(4,128)(2,1)}, u32[]{:S(2)}) copy-start(bf16[4,1024]{1,0:T(4,128)(2,1)} %param.29) | copy-start | bytes 24580
  35.5 178.7 %all-gather.11.cloned.1.call-start = ((), (), s32[]{:S(2)}) async-start(), calls=%async_computation.6 | async-start | bytes 6127616 | tf_op jit(solution)/shard_map/all_gather | solution.py:317
  36.3 209.6 %all-gather.13.cloned.1.call-start = ((), (), s32[]{:S(2)}) async-start(), calls=%async_computation.7 | async-start | bytes 3063808 | tf_op jit(solution)/shard_map/all_gather | solution.py:317
  43.6 48.8 %copy-start.8 = (bf16[1,256,1024]{2,1,0:T(8,128)(2,1)}, bf16[1,256,1024]{2,1,0:T(8,128)(2,1)S(1)}, u32[]{:S(2)}) copy-start(bf16[1,256,1024]{2,1,0:T(8,128)(2,1)S(1)} %all-gather) | copy-start | bytes 1572868
  44.6 429.0 %reduce-scatter.3.cloned.1.call-start = ((), (), s32[]{:S(2)}) async-start(), calls=%async_computation.8 | async-start | bytes 6963200 | tf_op jit(solution)/shard_map/reduce_scatter | solution.py:560
  92.4 6.6 %collective-permute-start = (bf16[3,2048]{1,0:T(4,128)(2,1)S(1)}, bf16[3,2048]{1,0:T(4,128)(2,1)S(1)}, u32[]{:S(2)}, u32[]{:S(2)}) collective-permute-start(bf16[3,2048]{1,0:T(4,128)(2,1)S(1)} %slice.261), channel_id=1, source_target_pairs={{0,4},{4,8},{8,12},{1,5},{5,9},{9,13},{2,6},{6,10},{10,14},{3,7},{... | collective-permute-start | bytes 36872 | tf_op jit(solution)/shard_map/ppermute | solution.py:19
  140.6 32.3 %copy-start.14 = (f32[4,1,128,256]{3,2,1,0:T(8,128)S(1)}, f32[4,1,128,256]{3,2,1,0:T(8,128)}, u32[]{:S(2)}) copy-start(f32[4,1,128,256]{3,2,1,0:T(8,128)} %get-tuple-element.35) | copy-start | bytes 1572868
  140.6 32.3 %copy-start.15 = (f32[4,1,128,128]{3,2,1,0:T(8,128)S(1)}, f32[4,1,128,128]{3,2,1,0:T(8,128)}, u32[]{:S(2)}) copy-start(f32[4,1,128,128]{3,2,1,0:T(8,128)} %get-tuple-element.36) | copy-start | bytes 786436
  140.6 41.4 %copy-start.38 = (bf16[1024]{0:T(1024)(128)(2,1)S(1)}, bf16[1024]{0:T(1024)(128)(2,1)}, u32[]{:S(2)}) copy-start(bf16[1024]{0:T(1024)(128)(2,1)} %param.32) | copy-start | bytes 6148
  141.7 14.6 %collective-permute-start.1 = (bf16[4,128,256]{2,1,0:T(8,128)(2,1)S(1)}, bf16[4,128,256]{2,1,0:T(8,128)(2,1)S(1)}, u32[]{:S(2)}, u32[]{:S(2)}) collective-permute-start(bf16[4,128,256]{2,1,0:T(8,128)(2,1)S(1)} %bitcast_convert_fusion.1), channel_id=1, source_target_pairs={{0,4},{4,8},{8,12},{1,5},{5,9},{9,13},{2,6},{6,10},{10,14},{3,7},{... | collective-permute-start | bytes 786440 | tf_op jit(solution)/shard_map/ppermute | solution.py:19
  157.8 15.0 %collective-permute-start.2 = (bf16[4,128,256]{2,1,0:T(8,128)(2,1)S(1)}, bf16[4,128,256]{2,1,0:T(8,128)(2,1)S(1)}, u32[]{:S(2)}, u32[]{:S(2)}) collective-permute-start(bf16[4,128,256]{2,1,0:T(8,128)(2,1)S(1)} %fusion.12), channel_id=1, source_target_pairs={{0,4},{4,8},{8,12},{1,5},{5,9},{9,13},{2,6},{6,10},{10,14},{3,7},{... | collective-permute-start | bytes 786440 | tf_op jit(solution)/shard_map/ppermute | solution.py:19
  173.3 18.8 %collective-permute-start.3 = (bf16[4,128,256]{2,1,0:T(8,128)(2,1)S(1)}, bf16[4,128,256]{2,1,0:T(8,128)(2,1)S(1)}, u32[]{:S(2)}, u32[]{:S(2)}) collective-permute-start(bf16[4,128,256]{2,1,0:T(8,128)(2,1)S(1)} %fusion.13), channel_id=1, source_target_pairs={{0,4},{4,8},{8,12},{1,5},{5,9},{9,13},{2,6},{6,10},{10,14},{3,7},{... | collective-permute-start | bytes 786440 | tf_op jit(solution)/shard_map/ppermute | solution.py:19
  200.0 13.8 %collective-permute-start.4 = (bf16[256,1024]{1,0:T(8,128)(2,1)S(1)}, bf16[256,1024]{1,0:T(8,128)(2,1)S(1)}, u32[]{:S(2)}, u32[]{:S(2)}) collective-permute-start(bf16[256,1024]{1,0:T(8,128)(2,1)S(1)} %convolution_convert_fusion.5), channel_id=1, source_target_pairs={{0,16},{16,0},{1,17},{17,1},{2,18},{18,2},{3,19},{19,3},{4,20},{20... | collective-permute-start | bytes 1572872 | tf_op jit(solution)/shard_map/ppermute | solution.py:325
  252.8 14.1 %collective-permute-start.6 = (bf16[256,1024]{1,0:T(8,128)(2,1)S(1)}, bf16[256,1024]{1,0:T(8,128)(2,1)S(1)}, u32[]{:S(2)}, u32[]{:S(2)}) collective-permute-start(bf16[256,1024]{1,0:T(8,128)(2,1)S(1)} %convolution_convert_fusion.6), channel_id=1, source_target_pairs={{0,16},{16,0},{1,17},{17,1},{2,18},{18,2},{3,19},{19,3},{4,20},{20... | collective-permute-start | bytes 1572872 | tf_op jit(solution)/shard_map/ppermute | solution.py:325
  278.1 9.5 %collective-permute-start.7 = (bf16[4,128,256]{2,1,0:T(8,128)(2,1)S(1)}, bf16[4,128,256]{2,1,0:T(8,128)(2,1)S(1)}, u32[]{:S(2)}, u32[]{:S(2)}) collective-permute-start(bf16[4,128,256]{2,1,0:T(8,128)(2,1)S(1)} %bitcast_convert_fusion), channel_id=1, source_target_pairs={{4,0},{8,4},{12,8},{5,1},{9,5},{13,9},{6,2},{10,6},{14,10},{7,3},{... | collective-permute-start | bytes 786440 | tf_op jit(solution)/shard_map/ppermute | solution.py:19
  289.1 8.6 %collective-permute-start.8 = (bf16[4,128,256]{2,1,0:T(8,128)(2,1)S(1)}, bf16[4,128,256]{2,1,0:T(8,128)(2,1)S(1)}, u32[]{:S(2)}, u32[]{:S(2)}) collective-permute-start(bf16[4,128,256]{2,1,0:T(8,128)(2,1)S(1)} %fusion.14), channel_id=1, source_target_pairs={{4,0},{8,4},{12,8},{5,1},{9,5},{13,9},{6,2},{10,6},{14,10},{7,3},{... | collective-permute-start | bytes 786440 | tf_op jit(solution)/shard_map/ppermute | solution.py:19
  298.1 8.3 %collective-permute-start.9 = (bf16[4,128,256]{2,1,0:T(8,128)(2,1)S(1)}, bf16[4,128,256]{2,1,0:T(8,128)(2,1)S(1)}, u32[]{:S(2)}, u32[]{:S(2)}) collective-permute-start(bf16[4,128,256]{2,1,0:T(8,128)(2,1)S(1)} %fusion.15), channel_id=1, source_target_pairs={{4,0},{8,4},{12,8},{5,1},{9,5},{13,9},{6,2},{10,6},{14,10},{7,3},{... | collective-permute-start | bytes 786440 | tf_op jit(solution)/shard_map/ppermute | solution.py:19
  346.7 5.8 %collective-permute-start.10 = (f32[3,2048]{1,0:T(4,128)S(1)}, f32[3,2048]{1,0:T(4,128)S(1)}, u32[]{:S(2)}, u32[]{:S(2)}) collective-permute-start(f32[3,2048]{1,0:T(4,128)S(1)} %pad_add_fusion.1), channel_id=1, source_target_pairs={{4,0},{8,4},{12,8},{5,1},{9,5},{13,9},{6,2},{10,6},{14,10},{7,3},{... | collective-permute-start | bytes 73736 | tf_op jit(solution)/shard_map/ppermute | solution.py:19
  358.3 210.0 %reduce-scatter.5.cloned.1.call-start = ((), (), s32[]{:S(2)}) async-start(), calls=%async_computation.9 | async-start | bytes 11419648 | tf_op jit(solution)/shard_map/reduce_scatter | solution.py:521
  386.7 6.4 %collective-permute-start.5 = (bf16[128,1024]{1,0:T(8,128)(2,1)S(1)}, bf16[128,1024]{1,0:T(8,128)(2,1)S(1)}, u32[]{:S(2)}, u32[]{:S(2)}) collective-permute-start(bf16[128,1024]{1,0:T(8,128)(2,1)S(1)} %dynamic-slice_convert_fusion.1), channel_id=1, source_target_pairs={{0,16},{16,0},{1,17},{17,1},{2,18},{18,2},{3,19},{19,3},{4,20},{20... | collective-permute-start | bytes 786440 | tf_op jit(solution)/shard_map/ppermute | solution.py:347
  400.6 6.4 %collective-permute-start.11 = (bf16[128,1024]{1,0:T(8,128)(2,1)S(1)}, bf16[128,1024]{1,0:T(8,128)(2,1)S(1)}, u32[]{:S(2)}, u32[]{:S(2)}) collective-permute-start(bf16[128,1024]{1,0:T(8,128)(2,1)S(1)} %dynamic-slice_convert_fusion), channel_id=1, source_target_pairs={{0,16},{16,0},{1,17},{17,1},{2,18},{18,2},{3,19},{19,3},{4,20},{20... | collective-permute-start | bytes 786440 | tf_op jit(solution)/shard_map/ppermute | solution.py:347
  407.3 3.7 collective-permute-start.12
  (37 other events, 282.1 us)
Sparse Core Ops, SparseCore 0:
  22.8 63.3 all-gather.6
  89.0 40.1 all-gather.8
  132.0 64.1 all-gather.10
  199.0 46.9 all-gather.12
  358.4 85.5 reduce-scatter.2
  447.9 120.3 reduce-scatter.4
